TPU v7x, 32 devices: a whole 2x2x4 slice. The times are simulated.
32 devices in a mesh: gx: 4 (over y, x), gy: 8 (over z, core).
Axes of the slice: x: 2, y: 2, z: 4, core: 2. Of those that a mesh axis runs over, the one named last changes fastest.
Arguments:
- velocity: float32 [3, 32, 128, 256], P(None, 'gx', 'gy'), may hold values from -6 to 6
- pressure: float32 [32, 128, 256], P('gx', 'gy'), may hold values from -4 to 4
- part_cell: int32 [4, 8, 8, 512], P('gx', 'gy'), may hold values from 0 to 32767
- part_count: int32 [4, 8, 8], P('gx', 'gy'), may hold values from 1 to 512, as said below
- grain_velocities: float32 [4, 8, 8, 3, 512], P('gx', 'gy'), may hold values from -6 to 6
- part_vol: float32 [4, 8, 8, 512], P('gx', 'gy'), may hold values from 0.05 to 0.3
Outputs:
- velocity_out: float32 [3, 32, 128, 256], P(None, 'gx', 'gy')
- pressure_out: float32 [32, 128, 256], P('gx', 'gy')
- drag: float32 [4, 8, 8, 3, 512], P('gx', 'gy')
Inputs may be any that keep to these rules, and one draw needn't show every extreme that they name: Every DEM owner (a, b) has at least one c with part_count[a, b, c] equal to 512.
All inputs are finite; a program needn't handle non-finite values.
Results may differ from a plain program's by a relative error of at most 0.00002.
Values sent between devices are 32-bit elements; how exact they have to be, the bound alone decides.
A program may use at most 128 MiB of HBM per device.

v0:
```python
import jax
import jax.numpy as jnp
from jax import lax
from jax.sharding import PartitionSpec as P

STEPS = 2
SWEEPS = 4
drag_coefficient = 2.0
time_step = 0.25
viscosity = 0.2
eps_floor = 0.4


def extended(block, sides, width):
    for axis, dim in sides:
        count = lax.axis_size(axis)
        forward = [(i, i + 1) for i in range(count - 1)]
        backward = [(target, source) for source, target in forward]
        low = lax.ppermute(
            lax.slice_in_dim(block, block.shape[dim] - width, None, axis=dim), axis, forward
        )
        high = lax.ppermute(lax.slice_in_dim(block, 0, width, axis=dim), axis, backward)
        block = jnp.concatenate([low, block, high], axis=dim)
    return block


def cell_faces(padded):
    return [
        padded[..., 2:, 1:-1, 1:-1],
        padded[..., :-2, 1:-1, 1:-1],
        padded[..., 1:-1, 2:, 1:-1],
        padded[..., 1:-1, :-2, 1:-1],
        padded[..., 1:-1, 1:-1, 2:],
        padded[..., 1:-1, 1:-1, :-2],
    ]


def padding_thickness(field):
    widths = [(0, 0)] * (field.ndim - 1) + [(1, 1)]
    return jnp.pad(field, widths)


def laplacian_operator(padded_velocity_field, flow_velocity, padded_voidage, porous_medium):
    near = cell_faces(padded_velocity_field)
    kernel_weights = cell_faces(padded_voidage)
    total = jnp.zeros_like(flow_velocity)
    for index in range(6):
        total = (
            total
            + 0.5
            * (porous_medium + kernel_weights[index])
            * (near[index] - flow_velocity)
            / porous_medium
        )
    return total


def divergence(flux_pad):
    near = cell_faces(flux_pad)
    return (
        0.5
        / time_step
        * (near[0][0] - near[1][0] + (near[2][1] - near[3][1]) + (near[4][2] - near[5][2]))
    )


def relaxation_terms(padded_pressure_field, padded_voidage):
    central_value = padded_voidage[1:-1, 1:-1, 1:-1]
    near = cell_faces(padded_pressure_field)
    kernel_weights = cell_faces(padded_voidage)
    numerator = jnp.zeros_like(central_value)
    denominator = jnp.zeros_like(central_value)
    for index in range(6):
        weight = 0.5 * (central_value + kernel_weights[index])
        numerator = numerator + weight * near[index]
        denominator = denominator + weight
    return (numerator, denominator)


def gradient(padded_pressure_field):
    near = cell_faces(padded_pressure_field)
    return jnp.stack(
        [0.5 * (near[0] - near[1]), 0.5 * (near[2] - near[3]), 0.5 * (near[4] - near[5])]
    )


def per_device(velocity, pressure, part_cell, part_count, grain_velocities, part_vol):
    rows_x, rows_y, depth = pressure.shape
    capacity = part_vol.shape[-1]
    grid_cells = rows_x * rows_y * depth
    slots = jnp.arange(capacity, dtype=jnp.int32)
    alive = slots[None, None, None, :] < part_count[..., None]
    grain_volume = jnp.where(alive, part_vol, jnp.float32(0.0))
    loads = jnp.concatenate([grain_velocities, grain_volume[..., None, :]], axis=3)
    got_cell = lax.all_to_all(part_cell, "gy", split_axis=2, concat_axis=2, tiled=True)
    got_load = lax.all_to_all(loads, "gy", split_axis=2, concat_axis=2, tiled=True)
    target_field = got_cell.reshape(-1)
    got_vol = got_load[..., 3, :]
    got_vel = got_load[..., :3, :]
    carried = jnp.moveaxis(got_vol[..., None, :] * got_vel, 3, 4).reshape(-1, 3)
    solid = jax.ops.segment_sum(got_vol.reshape(-1), target_field, num_segments=grid_cells).reshape(
        rows_x, rows_y, depth
    )
    mass_flux = jax.ops.segment_sum(carried, target_field, num_segments=grid_cells).T.reshape(
        3, rows_x, rows_y, depth
    )
    porous_medium = jnp.maximum(1.0 - solid, eps_floor)
    widened_field = extended(porous_medium, (("gx", 0), ("gy", 1)), 2)
    padded_voidage = padding_thickness(widened_field[1:-1, 1:-1])
    for step in range(STEPS):
        velocity_rotation = extended(velocity, (("gx", 1), ("gy", 2)), 1)
        spread_to_mesh = laplacian_operator(
            padding_thickness(velocity_rotation), velocity, padded_voidage, porous_medium
        )
        force = drag_coefficient * (mass_flux - solid * velocity) / porous_medium
        guess = velocity + time_step * (viscosity * spread_to_mesh + force)
        flux_cycle = extended(porous_medium * guess, (("gx", 1), ("gy", 2)), 1)
        source = divergence(padding_thickness(flux_cycle))
        for sweep in range(SWEEPS):
            pressure_rotation = extended(pressure, (("gx", 0), ("gy", 1)), 1)
            numerator, denominator = relaxation_terms(
                padding_thickness(pressure_rotation), padded_voidage
            )
            pressure = (numerator - source) / denominator
        slope_cycle = extended(pressure, (("gx", 0), ("gy", 1)), 1)
        velocity = guess - time_step * gradient(padding_thickness(slope_cycle))
    flat_vel = velocity.reshape(3, grid_cells)
    flattened_voids = porous_medium.reshape(grid_cells)
    slot_shape_factors = got_vol.shape
    cell_flow_speed = jnp.moveaxis(
        flat_vel[:, target_field].reshape((3,) + slot_shape_factors), 0, 3
    )
    cell_void_fraction = flattened_voids[target_field].reshape(slot_shape_factors)
    coupled_state = jnp.concatenate([cell_flow_speed, cell_void_fraction[..., None, :]], axis=3)
    back = lax.all_to_all(coupled_state, "gy", split_axis=2, concat_axis=2, tiled=True)
    drag = (
        grain_volume[..., None, :]
        * drag_coefficient
        * (back[..., :3, :] - grain_velocities)
        / back[..., 3:4, :]
    )
    return (velocity, pressure, drag)


def solution(mesh):
    placed = (
        P(None, "gx", "gy", None),
        P("gx", "gy", None),
        P("gx", "gy", None, None),
        P("gx", "gy", None),
        P("gx", "gy", None, None, None),
        P("gx", "gy", None, None),
    )
    return jax.shard_map(
        per_device,
        mesh=mesh,
        in_specs=placed,
        out_specs=(P(None, "gx", "gy", None), P("gx", "gy", None), P("gx", "gy", None, None, None)),
        check_vma=False,
    )
```

profile of v0, /device:TPU:4, one launch (start us, length us, event | category | flops | bytes accessed | tf_op | source)
XLA Modules:
  0.0 359.1 jit_solution(8799463692055073704)
XLA Ops:
  3.6 4.9 %all-to-all-start.1 = ((f32[1,1,8,4,512]{4,3,1,0,2:T(4,128)}), f32[1,1,8,4,512]{4,3,1,0,2:T(4,128)S(1)}, u32[]{:S(2)}, u32[]{:S(2)}) async-start(f32[1,1,8,4,512]{4,3,1,0,2:T(4,128)} %pad_maximum_fusion.104), calls=%async_computation.1 | async-start | bytes 131072 | tf_op jit(solution)/shard_map/all_to_all | solution.py:96
  9.2 3.4 collective-permute-start.9
  13.4 1.9 collective-permute-start.3
  15.4 4.8 %collective-permute-start.1 = (f32[3,1,16,256]{3,2,1,0:T(8,128)S(1)}, f32[3,1,16,256]{3,2,1,0:T(8,128)S(1)}, u32[]{:S(2)}, u32[]{:S(2)}) collective-permute-start(f32[3,1,16,256]{3,2,1,0:T(8,128)S(1)} %get-tuple-element.35), channel_id=1, source_target_pairs={{8,0},{16,8},{24,16},{9,1},{17,9},{25,17},{10,2},{18,10},{26,18},{... | collective-permute-start | bytes 147464 | tf_op jit(solution)/shard_map/ppermute | solution.py:22
  20.2 2.4 collective-permute-start.8
  25.9 5.1 %all-to-all-start = ((s32[1,1,8,512]{3,1,0,2:T(1,128)}), s32[1,1,8,512]{3,1,0,2:T(1,128)S(1)}, u32[]{:S(2)}, u32[]{:S(2)}) async-start(s32[1,1,8,512]{3,1,0,2:T(1,128)} %copy.25), calls=%async_computation | async-start | bytes 32768 | tf_op jit(solution)/shard_map/all_to_all | solution.py:95
  32.4 3.0 collective-permute-start.7
  36.7 21.9 %scatter_custom_fusion = f32[32768]{0:T(1024)S(1)} fusion(s32[4096]{0:T(1024)S(1)} %bitcast.52, f32[4096]{0:T(1024)S(1)} %bitcast.56, f32[]{:T(128)} %constant.10.clone.1), kind=kCustom, calls=%fused_computation.368 | custom fusion | flops 4096 | bytes 131076 | tf_op jit(solution)/shard_map/scatter-add | solution.py:101
  59.4 3.3 collective-permute-start
  62.8 2.5 collective-permute-start.2
  65.9 3.5 collective-permute-done.2
  70.8 3.0 collective-permute-start.6
  73.9 2.0 copy.29
  75.8 29.5 %scatter_custom_fusion.1 = f32[32768,3]{1,0:T(8,128)} fusion(s32[4096]{0:T(1024)S(1)} %bitcast.53, f32[4096,3]{1,0:T(8,128)} %copy.29, f32[]{:T(128)} %constant.10.clone.1), kind=kCustom, calls=%fused_computation.4 | custom fusion | flops 12288 | bytes 393728 | tf_op jit(solution)/shard_map/scatter-add | solution.py:104
  105.4 10.0 %copy.30 = f32[3,8,16,256]{3,2,1,0:T(8,128)S(1)} copy(f32[3,8,16,256]{0,3,2,1:T(8,128)} %bitcast.45) | data formatting | bytes 786432 | tf_op jit(solution)/shard_map/reshape | solution.py:104
  118.4 1.9 collective-permute-start.12
  120.3 3.9 %collective-permute-start.13 = (f32[3,1,16,256]{3,2,1,0:T(8,128)S(1)}, f32[3,1,16,256]{3,2,1,0:T(8,128)S(1)}, u32[]{:S(2)}, u32[]{:S(2)}) collective-permute-start(f32[3,1,16,256]{3,2,1,0:T(8,128)S(1)} %get-tuple-element.33), channel_id=1, source_target_pairs={{0,8},{8,16},{16,24},{1,9},{9,17},{17,25},{2,10},{10,18},{18,26},{... | collective-permute-start | bytes 147464 | tf_op jit(solution)/shard_map/ppermute | solution.py:19
  125.6 3.0 collective-permute-start.11
  130.0 4.0 %collective-permute-start.15 = (f32[3,10,1,256]{3,2,1,0:T(1,128)S(1)}, f32[3,10,1,256]{3,2,1,0:T(1,128)S(1)}, u32[]{:S(2)}, u32[]{:S(2)}) collective-permute-start(f32[3,10,1,256]{3,2,1,0:T(1,128)S(1)} %get-tuple-element.25), channel_id=1, source_target_pairs={{0,1},{1,2},{2,3},{3,4},{4,5},{5,6},{6,7},{8,9},{9,10},{10,11},{11... | collective-permute-start | bytes 92168 | tf_op jit(solution)/shard_map/ppermute | solution.py:19
  135.8 3.1 collective-permute-start.16
  139.0 2.7 collective-permute-start.17
  141.7 3.8 %collective-permute-done.17 = f32[1,16,256]{2,1,0:T(8,128)S(1)} collective-permute-done((f32[1,16,256]{2,1,0:T(8,128)S(1)}, f32[1,16,256]{2,1,0:T(8,128)S(1)}, u32[]{:S(2)}, u32[]{:S(2)}) %collective-permute-start.17) | collective-permute-done | bytes 16416 | tf_op jit(solution)/shard_map/ppermute | solution.py:19
  146.8 3.0 collective-permute-start.19
  151.1 1.9 collective-permute-start.20
  153.0 3.9 %collective-permute-start.21 = (f32[1,16,256]{2,1,0:T(8,128)S(1)}, f32[1,16,256]{2,1,0:T(8,128)S(1)}, u32[]{:S(2)}, u32[]{:S(2)}) collective-permute-start(f32[1,16,256]{2,1,0:T(8,128)S(1)} %get-tuple-element.77), channel_id=1, source_target_pairs={{0,8},{8,16},{16,24},{1,9},{9,17},{17,25},{2,10},{10,18},{18,26},{... | collective-permute-start | bytes 49160 | tf_op jit(solution)/shard_map/ppermute | solution.py:19
  156.9 2.6 collective-permute-done.21
  160.9 5.2 %collective-permute-start.23 = (f32[10,1,256]{2,1,0:T(1,128)S(1)}, f32[10,1,256]{2,1,0:T(1,128)S(1)}, u32[]{:S(2)}, u32[]{:S(2)}) collective-permute-start(f32[10,1,256]{2,1,0:T(1,128)S(1)} %get-tuple-element.57), channel_id=1, source_target_pairs={{0,1},{1,2},{2,3},{3,4},{4,5},{5,6},{6,7},{8,9},{9,10},{10,11},{11... | collective-permute-start | bytes 30728 | tf_op jit(solution)/shard_map/ppermute | solution.py:19
  167.2 1.9 collective-permute-start.24
  169.1 3.9 %collective-permute-start.25 = (f32[1,16,256]{2,1,0:T(8,128)S(1)}, f32[1,16,256]{2,1,0:T(8,128)S(1)}, u32[]{:S(2)}, u32[]{:S(2)}) collective-permute-start(f32[1,16,256]{2,1,0:T(8,128)S(1)} %get-tuple-element.75), channel_id=1, source_target_pairs={{0,8},{8,16},{16,24},{1,9},{9,17},{17,25},{2,10},{10,18},{18,26},{... | collective-permute-start | bytes 49160 | tf_op jit(solution)/shard_map/ppermute | solution.py:19
  173.0 2.6 collective-permute-done.25
  177.0 4.8 %collective-permute-start.27 = (f32[10,1,256]{2,1,0:T(1,128)S(1)}, f32[10,1,256]{2,1,0:T(1,128)S(1)}, u32[]{:S(2)}, u32[]{:S(2)}) collective-permute-start(f32[10,1,256]{2,1,0:T(1,128)S(1)} %get-tuple-element.55), channel_id=1, source_target_pairs={{0,1},{1,2},{2,3},{3,4},{4,5},{5,6},{6,7},{8,9},{9,10},{10,11},{11... | collective-permute-start | bytes 30728 | tf_op jit(solution)/shard_map/ppermute | solution.py:19
  183.0 1.9 collective-permute-start.28
  184.9 3.9 %collective-permute-start.29 = (f32[1,16,256]{2,1,0:T(8,128)S(1)}, f32[1,16,256]{2,1,0:T(8,128)S(1)}, u32[]{:S(2)}, u32[]{:S(2)}) collective-permute-start(f32[1,16,256]{2,1,0:T(8,128)S(1)} %get-tuple-element.73), channel_id=1, source_target_pairs={{0,8},{8,16},{16,24},{1,9},{9,17},{17,25},{2,10},{10,18},{18,26},{... | collective-permute-start | bytes 49160 | tf_op jit(solution)/shard_map/ppermute | solution.py:19
  188.8 2.6 collective-permute-done.29
  192.8 4.8 %collective-permute-start.31 = (f32[10,1,256]{2,1,0:T(1,128)S(1)}, f32[10,1,256]{2,1,0:T(1,128)S(1)}, u32[]{:S(2)}, u32[]{:S(2)}) collective-permute-start(f32[10,1,256]{2,1,0:T(1,128)S(1)} %get-tuple-element.53), channel_id=1, source_target_pairs={{0,1},{1,2},{2,3},{3,4},{4,5},{5,6},{6,7},{8,9},{9,10},{10,11},{11... | collective-permute-start | bytes 30728 | tf_op jit(solution)/shard_map/ppermute | solution.py:19
  198.9 1.9 collective-permute-start.32
  200.8 3.9 %collective-permute-start.33 = (f32[3,1,16,256]{3,2,1,0:T(8,128)S(1)}, f32[3,1,16,256]{3,2,1,0:T(8,128)S(1)}, u32[]{:S(2)}, u32[]{:S(2)}) collective-permute-start(f32[3,1,16,256]{3,2,1,0:T(8,128)S(1)} %get-tuple-element.31), channel_id=1, source_target_pairs={{0,8},{8,16},{16,24},{1,9},{9,17},{17,25},{2,10},{10,18},{18,26},{... | collective-permute-start | bytes 147464 | tf_op jit(solution)/shard_map/ppermute | solution.py:19
  204.9 2.8 collective-permute-done.33
  209.1 4.8 %collective-permute-start.35 = (f32[3,10,1,256]{3,2,1,0:T(1,128)S(1)}, f32[3,10,1,256]{3,2,1,0:T(1,128)S(1)}, u32[]{:S(2)}, u32[]{:S(2)}) collective-permute-start(f32[3,10,1,256]{3,2,1,0:T(1,128)S(1)} %get-tuple-element.23), channel_id=1, source_target_pairs={{0,1},{1,2},{2,3},{3,4},{4,5},{5,6},{6,7},{8,9},{9,10},{10,11},{11... | collective-permute-start | bytes 92168 | tf_op jit(solution)/shard_map/ppermute | solution.py:19
  215.9 1.9 collective-permute-start.36
  217.8 3.9 %collective-permute-start.37 = (f32[3,1,16,256]{3,2,1,0:T(8,128)S(1)}, f32[3,1,16,256]{3,2,1,0:T(8,128)S(1)}, u32[]{:S(2)}, u32[]{:S(2)}) collective-permute-start(f32[3,1,16,256]{3,2,1,0:T(8,128)S(1)} %get-tuple-element.29), channel_id=1, source_target_pairs={{0,8},{8,16},{16,24},{1,9},{9,17},{17,25},{2,10},{10,18},{18,26},{... | collective-permute-start | bytes 147464 | tf_op jit(solution)/shard_map/ppermute | solution.py:19
  221.9 2.8 collective-permute-done.37
  226.1 5.0 %collective-permute-start.39 = (f32[3,10,1,256]{3,2,1,0:T(1,128)S(1)}, f32[3,10,1,256]{3,2,1,0:T(1,128)S(1)}, u32[]{:S(2)}, u32[]{:S(2)}) collective-permute-start(f32[3,10,1,256]{3,2,1,0:T(1,128)S(1)} %get-tuple-element.21), channel_id=1, source_target_pairs={{0,1},{1,2},{2,3},{3,4},{4,5},{5,6},{6,7},{8,9},{9,10},{10,11},{11... | collective-permute-start | bytes 92168 | tf_op jit(solution)/shard_map/ppermute | solution.py:19
  232.8 1.9 collective-permute-start.40
  234.7 3.9 %collective-permute-start.41 = (f32[1,16,256]{2,1,0:T(8,128)S(1)}, f32[1,16,256]{2,1,0:T(8,128)S(1)}, u32[]{:S(2)}, u32[]{:S(2)}) collective-permute-start(f32[1,16,256]{2,1,0:T(8,128)S(1)} %get-tuple-element.71), channel_id=1, source_target_pairs={{0,8},{8,16},{16,24},{1,9},{9,17},{17,25},{2,10},{10,18},{18,26},{... | collective-permute-start | bytes 49160 | tf_op jit(solution)/shard_map/ppermute | solution.py:19
  238.6 2.6 collective-permute-done.41
  242.6 5.0 %collective-permute-start.43 = (f32[10,1,256]{2,1,0:T(1,128)S(1)}, f32[10,1,256]{2,1,0:T(1,128)S(1)}, u32[]{:S(2)}, u32[]{:S(2)}) collective-permute-start(f32[10,1,256]{2,1,0:T(1,128)S(1)} %get-tuple-element.49), channel_id=1, source_target_pairs={{0,1},{1,2},{2,3},{3,4},{4,5},{5,6},{6,7},{8,9},{9,10},{10,11},{11... | collective-permute-start | bytes 30728 | tf_op jit(solution)/shard_map/ppermute | solution.py:19
  248.8 1.9 collective-permute-start.44
  250.7 3.9 %collective-permute-start.45 = (f32[1,16,256]{2,1,0:T(8,128)S(1)}, f32[1,16,256]{2,1,0:T(8,128)S(1)}, u32[]{:S(2)}, u32[]{:S(2)}) collective-permute-start(f32[1,16,256]{2,1,0:T(8,128)S(1)} %get-tuple-element.69), channel_id=1, source_target_pairs={{0,8},{8,16},{16,24},{1,9},{9,17},{17,25},{2,10},{10,18},{18,26},{... | collective-permute-start | bytes 49160 | tf_op jit(solution)/shard_map/ppermute | solution.py:19
  254.7 2.6 collective-permute-done.45
  258.6 4.8 %collective-permute-start.47 = (f32[10,1,256]{2,1,0:T(1,128)S(1)}, f32[10,1,256]{2,1,0:T(1,128)S(1)}, u32[]{:S(2)}, u32[]{:S(2)}) collective-permute-start(f32[10,1,256]{2,1,0:T(1,128)S(1)} %get-tuple-element.47), channel_id=1, source_target_pairs={{0,1},{1,2},{2,3},{3,4},{4,5},{5,6},{6,7},{8,9},{9,10},{10,11},{11... | collective-permute-start | bytes 30728 | tf_op jit(solution)/shard_map/ppermute | solution.py:19
  264.7 1.9 collective-permute-start.48
  266.6 3.9 %collective-permute-start.49 = (f32[1,16,256]{2,1,0:T(8,128)S(1)}, f32[1,16,256]{2,1,0:T(8,128)S(1)}, u32[]{:S(2)}, u32[]{:S(2)}) collective-permute-start(f32[1,16,256]{2,1,0:T(8,128)S(1)} %get-tuple-element.67), channel_id=1, source_target_pairs={{0,8},{8,16},{16,24},{1,9},{9,17},{17,25},{2,10},{10,18},{18,26},{... | collective-permute-start | bytes 49160 | tf_op jit(solution)/shard_map/ppermute | solution.py:19
  270.5 2.6 collective-permute-done.49
  274.5 4.8 %collective-permute-start.51 = (f32[10,1,256]{2,1,0:T(1,128)S(1)}, f32[10,1,256]{2,1,0:T(1,128)S(1)}, u32[]{:S(2)}, u32[]{:S(2)}) collective-permute-start(f32[10,1,256]{2,1,0:T(1,128)S(1)} %get-tuple-element.45), channel_id=1, source_target_pairs={{0,1},{1,2},{2,3},{3,4},{4,5},{5,6},{6,7},{8,9},{9,10},{10,11},{11... | collective-permute-start | bytes 30728 | tf_op jit(solution)/shard_map/ppermute | solution.py:19
  280.5 1.9 collective-permute-start.52
  282.4 3.9 %collective-permute-start.53 = (f32[1,16,256]{2,1,0:T(8,128)S(1)}, f32[1,16,256]{2,1,0:T(8,128)S(1)}, u32[]{:S(2)}, u32[]{:S(2)}) collective-permute-start(f32[1,16,256]{2,1,0:T(8,128)S(1)} %get-tuple-element.65), channel_id=1, source_target_pairs={{0,8},{8,16},{16,24},{1,9},{9,17},{17,25},{2,10},{10,18},{18,26},{... | collective-permute-start | bytes 49160 | tf_op jit(solution)/shard_map/ppermute | solution.py:19
  286.4 2.6 collective-permute-done.53
  290.3 4.8 %collective-permute-start.55 = (f32[10,1,256]{2,1,0:T(1,128)S(1)}, f32[10,1,256]{2,1,0:T(1,128)S(1)}, u32[]{:S(2)}, u32[]{:S(2)}) collective-permute-start(f32[10,1,256]{2,1,0:T(1,128)S(1)} %get-tuple-element.43), channel_id=1, source_target_pairs={{0,1},{1,2},{2,3},{3,4},{4,5},{5,6},{6,7},{8,9},{9,10},{10,11},{11... | collective-permute-start | bytes 30728 | tf_op jit(solution)/shard_map/ppermute | solution.py:19
  295.1 23.0 %gather_fusion.1 = f32[4096]{0:T(1024)S(1)} fusion(f32[32768]{0:T(1024)S(1)} %subtract_maximum_fusion, s32[4096]{0:T(1024)S(1)} %broadcast_clamp_fusion), kind=kCustom, calls=%fused_computation.1 | custom fusion | bytes 49152 | tf_op jit(solution)/shard_map/gather | solution.py:133
  318.7 8.7 %copy.32 = f32[3,8,16,256]{0,3,2,1:T(8,128)} copy(f32[3,8,16,256]{3,2,1,0:T(8,128)S(1)} %fusion.54) | data formatting | bytes 786432 | tf_op jit(solution)/shard_map/sub | solution.py:126
  327.4 16.5 %gather_fusion = f32[4096,3]{1,0:T(8,128)S(1)} fusion(f32[3,32768]{0,1:T(8,128)} %bitcast.46, s32[4096]{0:T(1024)S(1)} %broadcast_clamp_fusion), kind=kCustom, calls=%fused_computation | custom fusion | bytes 114688 | tf_op jit(solution)/shard_map/gather | solution.py:131
  345.3 7.2 %all-to-all-start.2 = ((f32[1,1,8,4,512]{4,3,1,0,2:T(4,128)}), f32[1,1,8,4,512]{4,3,1,0,2:T(4,128)S(1)}, u32[]{:S(2)}, u32[]{:S(2)}) async-start(f32[1,1,8,4,512]{4,3,1,0,2:T(4,128)} %pad_maximum_fusion.105), calls=%async_computation.2 | async-start | bytes 131072 | tf_op jit(solution)/shard_map/all_to_all | solution.py:135
  352.5 5.9 %all-to-all-done.2 = f32[1,1,8,4,512]{4,3,1,0,2:T(4,128)S(1)} async-done(((f32[1,1,8,4,512]{4,3,1,0,2:T(4,128)}), f32[1,1,8,4,512]{4,3,1,0,2:T(4,128)S(1)}, u32[]{:S(2)}, u32[]{:S(2)}) %all-to-all-start.2) | async-done | bytes 65568 | tf_op jit(solution)/shard_map/all_to_all | solution.py:135
  (193 shorter events, 48.3 us)
Async XLA Ops:
  0.6 25.2 %copy-start.1 = (f32[3,8,16,256]{3,2,1,0:T(8,128)S(1)}, f32[3,8,16,256]{3,2,1,0:T(8,128)}, u32[]{:S(2)}) copy-start(f32[3,8,16,256]{3,2,1,0:T(8,128)} %param.6) | copy-start | bytes 1179652
  3.6 22.3 %all-to-all-start.1 = ((f32[1,1,8,4,512]{4,3,1,0,2:T(4,128)}), f32[1,1,8,4,512]{4,3,1,0,2:T(4,128)S(1)}, u32[]{:S(2)}, u32[]{:S(2)}) async-start(f32[1,1,8,4,512]{4,3,1,0,2:T(4,128)} %pad_maximum_fusion.104), calls=%async_computation.1 | async-start | bytes 131072 | tf_op jit(solution)/shard_map/all_to_all | solution.py:96
  9.2 14.8 %collective-permute-start.9 = (f32[1,16,256]{2,1,0:T(8,128)S(1)}, f32[1,16,256]{2,1,0:T(8,128)S(1)}, u32[]{:S(2)}, u32[]{:S(2)}) collective-permute-start(f32[1,16,256]{2,1,0:T(8,128)S(1)} %get-tuple-element.82), channel_id=1, source_target_pairs={{0,8},{8,16},{16,24},{1,9},{9,17},{17,25},{2,10},{10,18},{18,26},{... | collective-permute-start | bytes 49160 | tf_op jit(solution)/shard_map/ppermute | solution.py:19
  13.4 12.4 %collective-permute-start.3 = (f32[3,1,16,256]{3,2,1,0:T(8,128)S(1)}, f32[3,1,16,256]{3,2,1,0:T(8,128)S(1)}, u32[]{:S(2)}, u32[]{:S(2)}) collective-permute-start(f32[3,1,16,256]{3,2,1,0:T(8,128)S(1)} %get-tuple-element.36), channel_id=1, source_target_pairs={{0,8},{8,16},{16,24},{1,9},{9,17},{17,25},{2,10},{10,18},{18,26},{... | collective-permute-start | bytes 147464 | tf_op jit(solution)/shard_map/ppermute | solution.py:19
  15.4 10.5 %collective-permute-start.1 = (f32[3,1,16,256]{3,2,1,0:T(8,128)S(1)}, f32[3,1,16,256]{3,2,1,0:T(8,128)S(1)}, u32[]{:S(2)}, u32[]{:S(2)}) collective-permute-start(f32[3,1,16,256]{3,2,1,0:T(8,128)S(1)} %get-tuple-element.35), channel_id=1, source_target_pairs={{8,0},{16,8},{24,16},{9,1},{17,9},{25,17},{10,2},{18,10},{26,18},{... | collective-permute-start | bytes 147464 | tf_op jit(solution)/shard_map/ppermute | solution.py:22
  20.2 5.6 %collective-permute-start.8 = (f32[1,16,256]{2,1,0:T(8,128)S(1)}, f32[1,16,256]{2,1,0:T(8,128)S(1)}, u32[]{:S(2)}, u32[]{:S(2)}) collective-permute-start(f32[1,16,256]{2,1,0:T(8,128)S(1)} %get-tuple-element.81), channel_id=1, source_target_pairs={{8,0},{16,8},{24,16},{9,1},{17,9},{25,17},{10,2},{18,10},{26,18},{... | collective-permute-start | bytes 49160 | tf_op jit(solution)/shard_map/ppermute | solution.py:22
  25.8 40.1 %copy-start.5 = (f32[10,16,256]{2,1,0:T(8,128)}, f32[10,16,256]{2,1,0:T(8,128)S(1)}, u32[]{:S(2)}) copy-start(f32[10,16,256]{2,1,0:T(8,128)S(1)} %constant_dynamic-update-slice_fusion.3) | copy-start | bytes 491524
  25.9 33.5 %copy-start.8 = (f32[3,1,16,256]{3,2,1,0:T(8,128)}, f32[3,1,16,256]{3,2,1,0:T(8,128)S(1)}, u32[]{:S(2)}) copy-start(f32[3,1,16,256]{3,2,1,0:T(8,128)S(1)} %collective-permute-done.1) | copy-start | bytes 147460
  25.9 10.8 %all-to-all-start = ((s32[1,1,8,512]{3,1,0,2:T(1,128)}), s32[1,1,8,512]{3,1,0,2:T(1,128)S(1)}, u32[]{:S(2)}, u32[]{:S(2)}) async-start(s32[1,1,8,512]{3,1,0,2:T(1,128)} %copy.25), calls=%async_computation | async-start | bytes 32768 | tf_op jit(solution)/shard_map/all_to_all | solution.py:95
  31.1 34.2 %collective-permute-start.5 = (f32[3,10,1,256]{3,2,1,0:T(1,128)S(1)}, f32[3,10,1,256]{3,2,1,0:T(1,128)S(1)}, u32[]{:S(2)}, u32[]{:S(2)}) collective-permute-start(f32[3,10,1,256]{3,2,1,0:T(1,128)S(1)} %get-tuple-element.28), channel_id=1, source_target_pairs={{1,0},{2,1},{3,2},{4,3},{5,4},{6,5},{7,6},{9,8},{10,9},{11,10},{12... | collective-permute-start | bytes 92168 | tf_op jit(solution)/shard_map/ppermute | solution.py:22
  32.4 32.9 %collective-permute-start.7 = (f32[3,10,1,256]{3,2,1,0:T(1,128)S(1)}, f32[3,10,1,256]{3,2,1,0:T(1,128)S(1)}, u32[]{:S(2)}, u32[]{:S(2)}) collective-permute-start(f32[3,10,1,256]{3,2,1,0:T(1,128)S(1)} %get-tuple-element.27), channel_id=1, source_target_pairs={{0,1},{1,2},{2,3},{3,4},{4,5},{5,6},{6,7},{8,9},{9,10},{10,11},{11... | collective-permute-start | bytes 92168 | tf_op jit(solution)/shard_map/ppermute | solution.py:19
  36.7 39.1 %copy-start.22 = (s32[1,1,8,512]{3,1,0,2:T(1,128)}, s32[1,1,8,512]{3,1,0,2:T(1,128)S(1)}, u32[]{:S(2)}) copy-start(s32[1,1,8,512]{3,1,0,2:T(1,128)S(1)} %all-to-all-done) | copy-start | bytes 49156
  59.4 6.5 %collective-permute-start = (f32[2,16,256]{2,1,0:T(8,128)S(1)}, f32[2,16,256]{2,1,0:T(8,128)S(1)}, u32[]{:S(2)}, u32[]{:S(2)}) collective-permute-start(f32[2,16,256]{2,1,0:T(8,128)S(1)} %get-tuple-element.84), channel_id=1, source_target_pairs={{8,0},{16,8},{24,16},{9,1},{17,9},{25,17},{10,2},{18,10},{26,18},{... | collective-permute-start | bytes 98312 | tf_op jit(solution)/shard_map/ppermute | solution.py:22
  62.8 6.7 %collective-permute-start.2 = (f32[2,16,256]{2,1,0:T(8,128)S(1)}, f32[2,16,256]{2,1,0:T(8,128)S(1)}, u32[]{:S(2)}, u32[]{:S(2)}) collective-permute-start(f32[2,16,256]{2,1,0:T(8,128)S(1)} %get-tuple-element.83), channel_id=1, source_target_pairs={{0,8},{8,16},{16,24},{1,9},{9,17},{17,25},{2,10},{10,18},{18,26},{... | collective-permute-start | bytes 98312 | tf_op jit(solution)/shard_map/ppermute | solution.py:19
  69.5 45.9 %collective-permute-start.4 = (f32[12,2,256]{2,1,0:T(2,128)S(1)}, f32[12,2,256]{2,1,0:T(2,128)S(1)}, u32[]{:S(2)}, u32[]{:S(2)}) collective-permute-start(f32[12,2,256]{2,1,0:T(2,128)S(1)} %get-tuple-element.40), channel_id=1, source_target_pairs={{1,0},{2,1},{3,2},{4,3},{5,4},{6,5},{7,6},{9,8},{10,9},{11,10},{12... | collective-permute-start | bytes 73736 | tf_op jit(solution)/shard_map/ppermute | solution.py:22
  70.8 44.6 %collective-permute-start.6 = (f32[12,2,256]{2,1,0:T(2,128)S(1)}, f32[12,2,256]{2,1,0:T(2,128)S(1)}, u32[]{:S(2)}, u32[]{:S(2)}) collective-permute-start(f32[12,2,256]{2,1,0:T(2,128)S(1)} %get-tuple-element.39), channel_id=1, source_target_pairs={{0,1},{1,2},{2,3},{3,4},{4,5},{5,6},{6,7},{8,9},{9,10},{10,11},{11... | collective-permute-start | bytes 73736 | tf_op jit(solution)/shard_map/ppermute | solution.py:19
  118.4 10.2 %collective-permute-start.12 = (f32[3,1,16,256]{3,2,1,0:T(8,128)S(1)}, f32[3,1,16,256]{3,2,1,0:T(8,128)S(1)}, u32[]{:S(2)}, u32[]{:S(2)}) collective-permute-start(f32[3,1,16,256]{3,2,1,0:T(8,128)S(1)} %get-tuple-element.34), channel_id=1, source_target_pairs={{8,0},{16,8},{24,16},{9,1},{17,9},{25,17},{10,2},{18,10},{26,18},{... | collective-permute-start | bytes 147464 | tf_op jit(solution)/shard_map/ppermute | solution.py:22
  120.3 8.3 %collective-permute-start.13 = (f32[3,1,16,256]{3,2,1,0:T(8,128)S(1)}, f32[3,1,16,256]{3,2,1,0:T(8,128)S(1)}, u32[]{:S(2)}, u32[]{:S(2)}) collective-permute-start(f32[3,1,16,256]{3,2,1,0:T(8,128)S(1)} %get-tuple-element.33), channel_id=1, source_target_pairs={{0,8},{8,16},{16,24},{1,9},{9,17},{17,25},{2,10},{10,18},{18,26},{... | collective-permute-start | bytes 147464 | tf_op jit(solution)/shard_map/ppermute | solution.py:19
  124.3 9.8 %collective-permute-start.10 = (f32[10,1,256]{2,1,0:T(1,128)S(1)}, f32[10,1,256]{2,1,0:T(1,128)S(1)}, u32[]{:S(2)}, u32[]{:S(2)}) collective-permute-start(f32[10,1,256]{2,1,0:T(1,128)S(1)} %get-tuple-element.62), channel_id=1, source_target_pairs={{1,0},{2,1},{3,2},{4,3},{5,4},{6,5},{7,6},{9,8},{10,9},{11,10},{12... | collective-permute-start | bytes 30728 | tf_op jit(solution)/shard_map/ppermute | solution.py:22
  125.6 8.5 %collective-permute-start.11 = (f32[10,1,256]{2,1,0:T(1,128)S(1)}, f32[10,1,256]{2,1,0:T(1,128)S(1)}, u32[]{:S(2)}, u32[]{:S(2)}) collective-permute-start(f32[10,1,256]{2,1,0:T(1,128)S(1)} %get-tuple-element.61), channel_id=1, source_target_pairs={{0,1},{1,2},{2,3},{3,4},{4,5},{5,6},{6,7},{8,9},{9,10},{10,11},{11... | collective-permute-start | bytes 30728 | tf_op jit(solution)/shard_map/ppermute | solution.py:19
  128.7 5.6 %collective-permute-start.14 = (f32[3,10,1,256]{3,2,1,0:T(1,128)S(1)}, f32[3,10,1,256]{3,2,1,0:T(1,128)S(1)}, u32[]{:S(2)}, u32[]{:S(2)}) collective-permute-start(f32[3,10,1,256]{3,2,1,0:T(1,128)S(1)} %get-tuple-element.26), channel_id=1, source_target_pairs={{1,0},{2,1},{3,2},{4,3},{5,4},{6,5},{7,6},{9,8},{10,9},{11,10},{12... | collective-permute-start | bytes 92168 | tf_op jit(solution)/shard_map/ppermute | solution.py:22
  130.0 4.9 %collective-permute-start.15 = (f32[3,10,1,256]{3,2,1,0:T(1,128)S(1)}, f32[3,10,1,256]{3,2,1,0:T(1,128)S(1)}, u32[]{:S(2)}, u32[]{:S(2)}) collective-permute-start(f32[3,10,1,256]{3,2,1,0:T(1,128)S(1)} %get-tuple-element.25), channel_id=1, source_target_pairs={{0,1},{1,2},{2,3},{3,4},{4,5},{5,6},{6,7},{8,9},{9,10},{10,11},{11... | collective-permute-start | bytes 92168 | tf_op jit(solution)/shard_map/ppermute | solution.py:19
  135.8 5.9 %collective-permute-start.16 = (f32[1,16,256]{2,1,0:T(8,128)S(1)}, f32[1,16,256]{2,1,0:T(8,128)S(1)}, u32[]{:S(2)}, u32[]{:S(2)}) collective-permute-start(f32[1,16,256]{2,1,0:T(8,128)S(1)} %get-tuple-element.80), channel_id=1, source_target_pairs={{8,0},{16,8},{24,16},{9,1},{17,9},{25,17},{10,2},{18,10},{26,18},{... | collective-permute-start | bytes 49160 | tf_op jit(solution)/shard_map/ppermute | solution.py:22
  139.0 6.5 %collective-permute-start.17 = (f32[1,16,256]{2,1,0:T(8,128)S(1)}, f32[1,16,256]{2,1,0:T(8,128)S(1)}, u32[]{:S(2)}, u32[]{:S(2)}) collective-permute-start(f32[1,16,256]{2,1,0:T(8,128)S(1)} %get-tuple-element.79), channel_id=1, source_target_pairs={{0,8},{8,16},{16,24},{1,9},{9,17},{17,25},{2,10},{10,18},{18,26},{... | collective-permute-start | bytes 49160 | tf_op jit(solution)/shard_map/ppermute | solution.py:19
  145.5 4.3 %collective-permute-start.18 = (f32[10,1,256]{2,1,0:T(1,128)S(1)}, f32[10,1,256]{2,1,0:T(1,128)S(1)}, u32[]{:S(2)}, u32[]{:S(2)}) collective-permute-start(f32[10,1,256]{2,1,0:T(1,128)S(1)} %get-tuple-element.60), channel_id=1, source_target_pairs={{1,0},{2,1},{3,2},{4,3},{5,4},{6,5},{7,6},{9,8},{10,9},{11,10},{12... | collective-permute-start | bytes 30728 | tf_op jit(solution)/shard_map/ppermute | solution.py:22
  146.8 3.9 %collective-permute-start.19 = (f32[10,1,256]{2,1,0:T(1,128)S(1)}, f32[10,1,256]{2,1,0:T(1,128)S(1)}, u32[]{:S(2)}, u32[]{:S(2)}) collective-permute-start(f32[10,1,256]{2,1,0:T(1,128)S(1)} %get-tuple-element.59), channel_id=1, source_target_pairs={{0,1},{1,2},{2,3},{3,4},{4,5},{5,6},{6,7},{8,9},{9,10},{10,11},{11... | collective-permute-start | bytes 30728 | tf_op jit(solution)/shard_map/ppermute | solution.py:19
  151.1 5.9 %collective-permute-start.20 = (f32[1,16,256]{2,1,0:T(8,128)S(1)}, f32[1,16,256]{2,1,0:T(8,128)S(1)}, u32[]{:S(2)}, u32[]{:S(2)}) collective-permute-start(f32[1,16,256]{2,1,0:T(8,128)S(1)} %get-tuple-element.78), channel_id=1, source_target_pairs={{8,0},{16,8},{24,16},{9,1},{17,9},{25,17},{10,2},{18,10},{26,18},{... | collective-permute-start | bytes 49160 | tf_op jit(solution)/shard_map/ppermute | solution.py:22
  153.0 6.5 %collective-permute-start.21 = (f32[1,16,256]{2,1,0:T(8,128)S(1)}, f32[1,16,256]{2,1,0:T(8,128)S(1)}, u32[]{:S(2)}, u32[]{:S(2)}) collective-permute-start(f32[1,16,256]{2,1,0:T(8,128)S(1)} %get-tuple-element.77), channel_id=1, source_target_pairs={{0,8},{8,16},{16,24},{1,9},{9,17},{17,25},{2,10},{10,18},{18,26},{... | collective-permute-start | bytes 49160 | tf_op jit(solution)/shard_map/ppermute | solution.py:19
  159.6 6.6 %collective-permute-start.22 = (f32[10,1,256]{2,1,0:T(1,128)S(1)}, f32[10,1,256]{2,1,0:T(1,128)S(1)}, u32[]{:S(2)}, u32[]{:S(2)}) collective-permute-start(f32[10,1,256]{2,1,0:T(1,128)S(1)} %get-tuple-element.58), channel_id=1, source_target_pairs={{1,0},{2,1},{3,2},{4,3},{5,4},{6,5},{7,6},{9,8},{10,9},{11,10},{12... | collective-permute-start | bytes 30728 | tf_op jit(solution)/shard_map/ppermute | solution.py:22
  160.9 5.9 %collective-permute-start.23 = (f32[10,1,256]{2,1,0:T(1,128)S(1)}, f32[10,1,256]{2,1,0:T(1,128)S(1)}, u32[]{:S(2)}, u32[]{:S(2)}) collective-permute-start(f32[10,1,256]{2,1,0:T(1,128)S(1)} %get-tuple-element.57), channel_id=1, source_target_pairs={{0,1},{1,2},{2,3},{3,4},{4,5},{5,6},{6,7},{8,9},{9,10},{10,11},{11... | collective-permute-start | bytes 30728 | tf_op jit(solution)/shard_map/ppermute | solution.py:19
  167.2 5.9 %collective-permute-start.24 = (f32[1,16,256]{2,1,0:T(8,128)S(1)}, f32[1,16,256]{2,1,0:T(8,128)S(1)}, u32[]{:S(2)}, u32[]{:S(2)}) collective-permute-start(f32[1,16,256]{2,1,0:T(8,128)S(1)} %get-tuple-element.76), channel_id=1, source_target_pairs={{8,0},{16,8},{24,16},{9,1},{17,9},{25,17},{10,2},{18,10},{26,18},{... | collective-permute-start | bytes 49160 | tf_op jit(solution)/shard_map/ppermute | solution.py:22
  169.1 6.5 %collective-permute-start.25 = (f32[1,16,256]{2,1,0:T(8,128)S(1)}, f32[1,16,256]{2,1,0:T(8,128)S(1)}, u32[]{:S(2)}, u32[]{:S(2)}) collective-permute-start(f32[1,16,256]{2,1,0:T(8,128)S(1)} %get-tuple-element.75), channel_id=1, source_target_pairs={{0,8},{8,16},{16,24},{1,9},{9,17},{17,25},{2,10},{10,18},{18,26},{... | collective-permute-start | bytes 49160 | tf_op jit(solution)/shard_map/ppermute | solution.py:19
  175.7 6.1 %collective-permute-start.26 = (f32[10,1,256]{2,1,0:T(1,128)S(1)}, f32[10,1,256]{2,1,0:T(1,128)S(1)}, u32[]{:S(2)}, u32[]{:S(2)}) collective-permute-start(f32[10,1,256]{2,1,0:T(1,128)S(1)} %get-tuple-element.56), channel_id=1, source_target_pairs={{1,0},{2,1},{3,2},{4,3},{5,4},{6,5},{7,6},{9,8},{10,9},{11,10},{12... | collective-permute-start | bytes 30728 | tf_op jit(solution)/shard_map/ppermute | solution.py:22
  177.0 5.6 %collective-permute-start.27 = (f32[10,1,256]{2,1,0:T(1,128)S(1)}, f32[10,1,256]{2,1,0:T(1,128)S(1)}, u32[]{:S(2)}, u32[]{:S(2)}) collective-permute-start(f32[10,1,256]{2,1,0:T(1,128)S(1)} %get-tuple-element.55), channel_id=1, source_target_pairs={{0,1},{1,2},{2,3},{3,4},{4,5},{5,6},{6,7},{8,9},{9,10},{10,11},{11... | collective-permute-start | bytes 30728 | tf_op jit(solution)/shard_map/ppermute | solution.py:19
  183.0 5.9 %collective-permute-start.28 = (f32[1,16,256]{2,1,0:T(8,128)S(1)}, f32[1,16,256]{2,1,0:T(8,128)S(1)}, u32[]{:S(2)}, u32[]{:S(2)}) collective-permute-start(f32[1,16,256]{2,1,0:T(8,128)S(1)} %get-tuple-element.74), channel_id=1, source_target_pairs={{8,0},{16,8},{24,16},{9,1},{17,9},{25,17},{10,2},{18,10},{26,18},{... | collective-permute-start | bytes 49160 | tf_op jit(solution)/shard_map/ppermute | solution.py:22
  184.9 6.5 %collective-permute-start.29 = (f32[1,16,256]{2,1,0:T(8,128)S(1)}, f32[1,16,256]{2,1,0:T(8,128)S(1)}, u32[]{:S(2)}, u32[]{:S(2)}) collective-permute-start(f32[1,16,256]{2,1,0:T(8,128)S(1)} %get-tuple-element.73), channel_id=1, source_target_pairs={{0,8},{8,16},{16,24},{1,9},{9,17},{17,25},{2,10},{10,18},{18,26},{... | collective-permute-start | bytes 49160 | tf_op jit(solution)/shard_map/ppermute | solution.py:19
  191.5 6.1 %collective-permute-start.30 = (f32[10,1,256]{2,1,0:T(1,128)S(1)}, f32[10,1,256]{2,1,0:T(1,128)S(1)}, u32[]{:S(2)}, u32[]{:S(2)}) collective-permute-start(f32[10,1,256]{2,1,0:T(1,128)S(1)} %get-tuple-element.54), channel_id=1, source_target_pairs={{1,0},{2,1},{3,2},{4,3},{5,4},{6,5},{7,6},{9,8},{10,9},{11,10},{12... | collective-permute-start | bytes 30728 | tf_op jit(solution)/shard_map/ppermute | solution.py:22
  192.8 5.6 %collective-permute-start.31 = (f32[10,1,256]{2,1,0:T(1,128)S(1)}, f32[10,1,256]{2,1,0:T(1,128)S(1)}, u32[]{:S(2)}, u32[]{:S(2)}) collective-permute-start(f32[10,1,256]{2,1,0:T(1,128)S(1)} %get-tuple-element.53), channel_id=1, source_target_pairs={{0,1},{1,2},{2,3},{3,4},{4,5},{5,6},{6,7},{8,9},{9,10},{10,11},{11... | collective-permute-start | bytes 30728 | tf_op jit(solution)/shard_map/ppermute | solution.py:19
  198.9 6.0 %collective-permute-start.32 = (f32[3,1,16,256]{3,2,1,0:T(8,128)S(1)}, f32[3,1,16,256]{3,2,1,0:T(8,128)S(1)}, u32[]{:S(2)}, u32[]{:S(2)}) collective-permute-start(f32[3,1,16,256]{3,2,1,0:T(8,128)S(1)} %get-tuple-element.32), channel_id=1, source_target_pairs={{8,0},{16,8},{24,16},{9,1},{17,9},{25,17},{10,2},{18,10},{26,18},{... | collective-permute-start | bytes 147464 | tf_op jit(solution)/shard_map/ppermute | solution.py:22
  200.8 6.9 %collective-permute-start.33 = (f32[3,1,16,256]{3,2,1,0:T(8,128)S(1)}, f32[3,1,16,256]{3,2,1,0:T(8,128)S(1)}, u32[]{:S(2)}, u32[]{:S(2)}) collective-permute-start(f32[3,1,16,256]{3,2,1,0:T(8,128)S(1)} %get-tuple-element.31), channel_id=1, source_target_pairs={{0,8},{8,16},{16,24},{1,9},{9,17},{17,25},{2,10},{10,18},{18,26},{... | collective-permute-start | bytes 147464 | tf_op jit(solution)/shard_map/ppermute | solution.py:19
  207.8 6.1 %collective-permute-start.34 = (f32[3,10,1,256]{3,2,1,0:T(1,128)S(1)}, f32[3,10,1,256]{3,2,1,0:T(1,128)S(1)}, u32[]{:S(2)}, u32[]{:S(2)}) collective-permute-start(f32[3,10,1,256]{3,2,1,0:T(1,128)S(1)} %get-tuple-element.24), channel_id=1, source_target_pairs={{1,0},{2,1},{3,2},{4,3},{5,4},{6,5},{7,6},{9,8},{10,9},{11,10},{12... | collective-permute-start | bytes 92168 | tf_op jit(solution)/shard_map/ppermute | solution.py:22
  209.1 5.6 %collective-permute-start.35 = (f32[3,10,1,256]{3,2,1,0:T(1,128)S(1)}, f32[3,10,1,256]{3,2,1,0:T(1,128)S(1)}, u32[]{:S(2)}, u32[]{:S(2)}) collective-permute-start(f32[3,10,1,256]{3,2,1,0:T(1,128)S(1)} %get-tuple-element.23), channel_id=1, source_target_pairs={{0,1},{1,2},{2,3},{3,4},{4,5},{5,6},{6,7},{8,9},{9,10},{10,11},{11... | collective-permute-start | bytes 92168 | tf_op jit(solution)/shard_map/ppermute | solution.py:19
  215.9 6.0 %collective-permute-start.36 = (f32[3,1,16,256]{3,2,1,0:T(8,128)S(1)}, f32[3,1,16,256]{3,2,1,0:T(8,128)S(1)}, u32[]{:S(2)}, u32[]{:S(2)}) collective-permute-start(f32[3,1,16,256]{3,2,1,0:T(8,128)S(1)} %get-tuple-element.30), channel_id=1, source_target_pairs={{8,0},{16,8},{24,16},{9,1},{17,9},{25,17},{10,2},{18,10},{26,18},{... | collective-permute-start | bytes 147464 | tf_op jit(solution)/shard_map/ppermute | solution.py:22
  217.8 6.9 %collective-permute-start.37 = (f32[3,1,16,256]{3,2,1,0:T(8,128)S(1)}, f32[3,1,16,256]{3,2,1,0:T(8,128)S(1)}, u32[]{:S(2)}, u32[]{:S(2)}) collective-permute-start(f32[3,1,16,256]{3,2,1,0:T(8,128)S(1)} %get-tuple-element.29), channel_id=1, source_target_pairs={{0,8},{8,16},{16,24},{1,9},{9,17},{17,25},{2,10},{10,18},{18,26},{... | collective-permute-start | bytes 147464 | tf_op jit(solution)/shard_map/ppermute | solution.py:19
  224.8 6.3 %collective-permute-start.38 = (f32[3,10,1,256]{3,2,1,0:T(1,128)S(1)}, f32[3,10,1,256]{3,2,1,0:T(1,128)S(1)}, u32[]{:S(2)}, u32[]{:S(2)}) collective-permute-start(f32[3,10,1,256]{3,2,1,0:T(1,128)S(1)} %get-tuple-element.22), channel_id=1, source_target_pairs={{1,0},{2,1},{3,2},{4,3},{5,4},{6,5},{7,6},{9,8},{10,9},{11,10},{12... | collective-permute-start | bytes 92168 | tf_op jit(solution)/shard_map/ppermute | solution.py:22
  226.1 5.8 %collective-permute-start.39 = (f32[3,10,1,256]{3,2,1,0:T(1,128)S(1)}, f32[3,10,1,256]{3,2,1,0:T(1,128)S(1)}, u32[]{:S(2)}, u32[]{:S(2)}) collective-permute-start(f32[3,10,1,256]{3,2,1,0:T(1,128)S(1)} %get-tuple-element.21), channel_id=1, source_target_pairs={{0,1},{1,2},{2,3},{3,4},{4,5},{5,6},{6,7},{8,9},{9,10},{10,11},{11... | collective-permute-start | bytes 92168 | tf_op jit(solution)/shard_map/ppermute | solution.py:19
  232.8 5.9 %collective-permute-start.40 = (f32[1,16,256]{2,1,0:T(8,128)S(1)}, f32[1,16,256]{2,1,0:T(8,128)S(1)}, u32[]{:S(2)}, u32[]{:S(2)}) collective-permute-start(f32[1,16,256]{2,1,0:T(8,128)S(1)} %get-tuple-element.72), channel_id=1, source_target_pairs={{8,0},{16,8},{24,16},{9,1},{17,9},{25,17},{10,2},{18,10},{26,18},{... | collective-permute-start | bytes 49160 | tf_op jit(solution)/shard_map/ppermute | solution.py:22
  234.7 6.5 %collective-permute-start.41 = (f32[1,16,256]{2,1,0:T(8,128)S(1)}, f32[1,16,256]{2,1,0:T(8,128)S(1)}, u32[]{:S(2)}, u32[]{:S(2)}) collective-permute-start(f32[1,16,256]{2,1,0:T(8,128)S(1)} %get-tuple-element.71), channel_id=1, source_target_pairs={{0,8},{8,16},{16,24},{1,9},{9,17},{17,25},{2,10},{10,18},{18,26},{... | collective-permute-start | bytes 49160 | tf_op jit(solution)/shard_map/ppermute | solution.py:19
  241.3 6.3 %collective-permute-start.42 = (f32[10,1,256]{2,1,0:T(1,128)S(1)}, f32[10,1,256]{2,1,0:T(1,128)S(1)}, u32[]{:S(2)}, u32[]{:S(2)}) collective-permute-start(f32[10,1,256]{2,1,0:T(1,128)S(1)} %get-tuple-element.50), channel_id=1, source_target_pairs={{1,0},{2,1},{3,2},{4,3},{5,4},{6,5},{7,6},{9,8},{10,9},{11,10},{12... | collective-permute-start | bytes 30728 | tf_op jit(solution)/shard_map/ppermute | solution.py:22
  242.6 5.8 %collective-permute-start.43 = (f32[10,1,256]{2,1,0:T(1,128)S(1)}, f32[10,1,256]{2,1,0:T(1,128)S(1)}, u32[]{:S(2)}, u32[]{:S(2)}) collective-permute-start(f32[10,1,256]{2,1,0:T(1,128)S(1)} %get-tuple-element.49), channel_id=1, source_target_pairs={{0,1},{1,2},{2,3},{3,4},{4,5},{5,6},{6,7},{8,9},{9,10},{10,11},{11... | collective-permute-start | bytes 30728 | tf_op jit(solution)/shard_map/ppermute | solution.py:19
  248.8 5.9 %collective-permute-start.44 = (f32[1,16,256]{2,1,0:T(8,128)S(1)}, f32[1,16,256]{2,1,0:T(8,128)S(1)}, u32[]{:S(2)}, u32[]{:S(2)}) collective-permute-start(f32[1,16,256]{2,1,0:T(8,128)S(1)} %get-tuple-element.70), channel_id=1, source_target_pairs={{8,0},{16,8},{24,16},{9,1},{17,9},{25,17},{10,2},{18,10},{26,18},{... | collective-permute-start | bytes 49160 | tf_op jit(solution)/shard_map/ppermute | solution.py:22
  250.7 6.5 %collective-permute-start.45 = (f32[1,16,256]{2,1,0:T(8,128)S(1)}, f32[1,16,256]{2,1,0:T(8,128)S(1)}, u32[]{:S(2)}, u32[]{:S(2)}) collective-permute-start(f32[1,16,256]{2,1,0:T(8,128)S(1)} %get-tuple-element.69), channel_id=1, source_target_pairs={{0,8},{8,16},{16,24},{1,9},{9,17},{17,25},{2,10},{10,18},{18,26},{... | collective-permute-start | bytes 49160 | tf_op jit(solution)/shard_map/ppermute | solution.py:19
  257.3 6.1 %collective-permute-start.46 = (f32[10,1,256]{2,1,0:T(1,128)S(1)}, f32[10,1,256]{2,1,0:T(1,128)S(1)}, u32[]{:S(2)}, u32[]{:S(2)}) collective-permute-start(f32[10,1,256]{2,1,0:T(1,128)S(1)} %get-tuple-element.48), channel_id=1, source_target_pairs={{1,0},{2,1},{3,2},{4,3},{5,4},{6,5},{7,6},{9,8},{10,9},{11,10},{12... | collective-permute-start | bytes 30728 | tf_op jit(solution)/shard_map/ppermute | solution.py:22
  258.6 5.6 %collective-permute-start.47 = (f32[10,1,256]{2,1,0:T(1,128)S(1)}, f32[10,1,256]{2,1,0:T(1,128)S(1)}, u32[]{:S(2)}, u32[]{:S(2)}) collective-permute-start(f32[10,1,256]{2,1,0:T(1,128)S(1)} %get-tuple-element.47), channel_id=1, source_target_pairs={{0,1},{1,2},{2,3},{3,4},{4,5},{5,6},{6,7},{8,9},{9,10},{10,11},{11... | collective-permute-start | bytes 30728 | tf_op jit(solution)/shard_map/ppermute | solution.py:19
  264.7 5.9 %collective-permute-start.48 = (f32[1,16,256]{2,1,0:T(8,128)S(1)}, f32[1,16,256]{2,1,0:T(8,128)S(1)}, u32[]{:S(2)}, u32[]{:S(2)}) collective-permute-start(f32[1,16,256]{2,1,0:T(8,128)S(1)} %get-tuple-element.68), channel_id=1, source_target_pairs={{8,0},{16,8},{24,16},{9,1},{17,9},{25,17},{10,2},{18,10},{26,18},{... | collective-permute-start | bytes 49160 | tf_op jit(solution)/shard_map/ppermute | solution.py:22
  266.6 6.5 %collective-permute-start.49 = (f32[1,16,256]{2,1,0:T(8,128)S(1)}, f32[1,16,256]{2,1,0:T(8,128)S(1)}, u32[]{:S(2)}, u32[]{:S(2)}) collective-permute-start(f32[1,16,256]{2,1,0:T(8,128)S(1)} %get-tuple-element.67), channel_id=1, source_target_pairs={{0,8},{8,16},{16,24},{1,9},{9,17},{17,25},{2,10},{10,18},{18,26},{... | collective-permute-start | bytes 49160 | tf_op jit(solution)/shard_map/ppermute | solution.py:19
  273.2 6.1 %collective-permute-start.50 = (f32[10,1,256]{2,1,0:T(1,128)S(1)}, f32[10,1,256]{2,1,0:T(1,128)S(1)}, u32[]{:S(2)}, u32[]{:S(2)}) collective-permute-start(f32[10,1,256]{2,1,0:T(1,128)S(1)} %get-tuple-element.46), channel_id=1, source_target_pairs={{1,0},{2,1},{3,2},{4,3},{5,4},{6,5},{7,6},{9,8},{10,9},{11,10},{12... | collective-permute-start | bytes 30728 | tf_op jit(solution)/shard_map/ppermute | solution.py:22
  274.5 5.6 %collective-permute-start.51 = (f32[10,1,256]{2,1,0:T(1,128)S(1)}, f32[10,1,256]{2,1,0:T(1,128)S(1)}, u32[]{:S(2)}, u32[]{:S(2)}) collective-permute-start(f32[10,1,256]{2,1,0:T(1,128)S(1)} %get-tuple-element.45), channel_id=1, source_target_pairs={{0,1},{1,2},{2,3},{3,4},{4,5},{5,6},{6,7},{8,9},{9,10},{10,11},{11... | collective-permute-start | bytes 30728 | tf_op jit(solution)/shard_map/ppermute | solution.py:19
  280.5 38.1 %copy-start = (f32[8,16,256]{2,1,0:T(8,128)}, f32[8,16,256]{2,1,0:T(8,128)S(1)}, u32[]{:S(2)}) copy-start(f32[8,16,256]{2,1,0:T(8,128)S(1)} %fusion.66) | copy-start | bytes 393220
  280.5 5.9 %collective-permute-start.52 = (f32[1,16,256]{2,1,0:T(8,128)S(1)}, f32[1,16,256]{2,1,0:T(8,128)S(1)}, u32[]{:S(2)}, u32[]{:S(2)}) collective-permute-start(f32[1,16,256]{2,1,0:T(8,128)S(1)} %get-tuple-element.66), channel_id=1, source_target_pairs={{8,0},{16,8},{24,16},{9,1},{17,9},{25,17},{10,2},{18,10},{26,18},{... | collective-permute-start | bytes 49160 | tf_op jit(solution)/shard_map/ppermute | solution.py:22
  282.4 6.5 %collective-permute-start.53 = (f32[1,16,256]{2,1,0:T(8,128)S(1)}, f32[1,16,256]{2,1,0:T(8,128)S(1)}, u32[]{:S(2)}, u32[]{:S(2)}) collective-permute-start(f32[1,16,256]{2,1,0:T(8,128)S(1)} %get-tuple-element.65), channel_id=1, source_target_pairs={{0,8},{8,16},{16,24},{1,9},{9,17},{17,25},{2,10},{10,18},{18,26},{... | collective-permute-start | bytes 49160 | tf_op jit(solution)/shard_map/ppermute | solution.py:19
  289.0 29.2 %collective-permute-start.54 = (f32[10,1,256]{2,1,0:T(1,128)S(1)}, f32[10,1,256]{2,1,0:T(1,128)S(1)}, u32[]{:S(2)}, u32[]{:S(2)}) collective-permute-start(f32[10,1,256]{2,1,0:T(1,128)S(1)} %get-tuple-element.44), channel_id=1, source_target_pairs={{1,0},{2,1},{3,2},{4,3},{5,4},{6,5},{7,6},{9,8},{10,9},{11,10},{12... | collective-permute-start | bytes 30728 | tf_op jit(solution)/shard_map/ppermute | solution.py:22
  290.3 27.9 %collective-permute-start.55 = (f32[10,1,256]{2,1,0:T(1,128)S(1)}, f32[10,1,256]{2,1,0:T(1,128)S(1)}, u32[]{:S(2)}, u32[]{:S(2)}) collective-permute-start(f32[10,1,256]{2,1,0:T(1,128)S(1)} %get-tuple-element.43), channel_id=1, source_target_pairs={{0,1},{1,2},{2,3},{3,4},{4,5},{5,6},{6,7},{8,9},{9,10},{10,11},{11... | collective-permute-start | bytes 30728 | tf_op jit(solution)/shard_map/ppermute | solution.py:19
  345.3 13.1 %all-to-all-start.2 = ((f32[1,1,8,4,512]{4,3,1,0,2:T(4,128)}), f32[1,1,8,4,512]{4,3,1,0,2:T(4,128)S(1)}, u32[]{:S(2)}, u32[]{:S(2)}) async-start(f32[1,1,8,4,512]{4,3,1,0,2:T(4,128)} %pad_maximum_fusion.105), calls=%async_computation.2 | async-start | bytes 131072 | tf_op jit(solution)/shard_map/all_to_all | solution.py:135
  (19 other events, 129.7 us)
where the time goes:
time: 361 us; the launch traced here: 359 us
  starting transfers between devices  178 us (49%)
  local copies, waits for them, and re-layouts  68.4 us (19%)
  other arithmetic  63.4 us (18%)
  waiting for transfers between devices  47.2 us (13%)
    ppermute x28, starting transfers between devices, extended(): lax.ppermute(lax.slice_in_dim(block, block.shape[dim] - width, None, axis...  110 us
    ppermute x28, starting transfers between devices, extended(): lax.ppermute(lax.slice_in_dim(block, 0, width, axis=dim), axis, backward)  51.1 us
    ppermute x28, waiting for transfers between devices, extended(): lax.ppermute(lax.slice_in_dim(block, block.shape[dim] - width, None, axis...  38.8 us
    scatter-add x1, other arithmetic, per_device(): jax.ops.segment_sum(carried, target_field, num_segments=grid_cells)  29.5 us
    gather x1, local copies, waits for them, and re-layouts, per_device(): flattened_voids[target_field].reshape(slot_shape_factors)  23 us
    scatter-add x1, other arithmetic, per_device(): jax.ops.segment_sum(got_vol.reshape(-1), target_field, num_segments=grid_...  21.9 us
    gather x1, local copies, waits for them, and re-layouts, per_device(): flat_vel[:, target_field].reshape((3,) + slot_shape_factors)  16.5 us
    reshape x1, local copies, waits for them, and re-layouts, per_device(): jax.ops.segment_sum(carried, target_field, num_segments=grid_cells)  9.97 us
  transfers between devices with their start and end apart: 59, of which 26 were waited for; matrix products, arithmetic and copies ran while one was open for 25% of the time, Pallas kernels for 0%

commit v1 on v0

--- a/solution.py
+++ b/solution.py
@@ -132,7 +132,12 @@
     )
     cell_void_fraction = flattened_voids[target_field].reshape(slot_shape_factors)
     coupled_state = jnp.concatenate([cell_flow_speed, cell_void_fraction[..., None, :]], axis=3)
-    back = lax.all_to_all(coupled_state, "gy", split_axis=2, concat_axis=2, tiled=True)
+    back = jnp.concatenate(
+        lax.all_to_all(
+            jnp.stack(jnp.split(coupled_state, lax.axis_size("gy"), axis=2)), "gy", 0, 0
+        ),
+        axis=2,
+    )
     drag = (
         grain_volume[..., None, :]
         * drag_coefficient

time: 361 us -> 366 us (1.014)
  other arithmetic: 63.4 us -> 67.5 us
    unnamed x0 -> x7, other arithmetic: none -> 4.23 us
where the time goes in v1:
time: 366 us; the launch traced here: 363 us
  starting transfers between devices  178 us (49%)
  local copies, waits for them, and re-layouts  68.4 us (19%)
  other arithmetic  67.5 us (18%)
  waiting for transfers between devices  47.2 us (13%)
    ppermute x28, starting transfers between devices, extended(): lax.ppermute(lax.slice_in_dim(block, block.shape[dim] - width, None, axis...  110 us
    ppermute x28, starting transfers between devices, extended(): lax.ppermute(lax.slice_in_dim(block, 0, width, axis=dim), axis, backward)  51.1 us
    ppermute x28, waiting for transfers between devices, extended(): lax.ppermute(lax.slice_in_dim(block, block.shape[dim] - width, None, axis...  38.8 us
    scatter-add x1, other arithmetic, per_device(): jax.ops.segment_sum(carried, target_field, num_segments=grid_cells)  29.5 us
    gather x1, local copies, waits for them, and re-layouts, per_device(): flattened_voids[target_field].reshape(slot_shape_factors)  23 us
    scatter-add x1, other arithmetic, per_device(): jax.ops.segment_sum(got_vol.reshape(-1), target_field, num_segments=grid_...  21.9 us
    gather x1, local copies, waits for them, and re-layouts, per_device(): flat_vel[:, target_field].reshape((3,) + slot_shape_factors)  16.5 us
    reshape x1, local copies, waits for them, and re-layouts, per_device(): jax.ops.segment_sum(carried, target_field, num_segments=grid_cells)  9.97 us
  transfers between devices with their start and end apart: 59, of which 26 were waited for; matrix products, arithmetic and copies ran while one was open for 25% of the time, Pallas kernels for 0%

profile of v1, /device:TPU:4, one launch (start us, length us, event | category | flops | bytes accessed | tf_op | source)
XLA Modules:
  0.0 363.3 jit_solution(13596238236922394150)
XLA Ops:
  3.6 4.9 %all-to-all-start.1 = ((f32[1,1,8,4,512]{4,3,1,0,2:T(4,128)}), f32[1,1,8,4,512]{4,3,1,0,2:T(4,128)S(1)}, u32[]{:S(2)}, u32[]{:S(2)}) async-start(f32[1,1,8,4,512]{4,3,1,0,2:T(4,128)} %pad_maximum_fusion.104), calls=%async_computation.1 | async-start | bytes 131072 | tf_op jit(solution)/shard_map/all_to_all | solution.py:96
  9.2 3.4 collective-permute-start.9
  13.4 1.9 collective-permute-start.3
  15.4 4.8 %collective-permute-start.1 = (f32[3,1,16,256]{3,2,1,0:T(8,128)S(1)}, f32[3,1,16,256]{3,2,1,0:T(8,128)S(1)}, u32[]{:S(2)}, u32[]{:S(2)}) collective-permute-start(f32[3,1,16,256]{3,2,1,0:T(8,128)S(1)} %get-tuple-element.35), channel_id=1, source_target_pairs={{8,0},{16,8},{24,16},{9,1},{17,9},{25,17},{10,2},{18,10},{26,18},{... | collective-permute-start | bytes 147464 | tf_op jit(solution)/shard_map/ppermute | solution.py:22
  20.2 2.4 collective-permute-start.8
  25.9 5.1 %all-to-all-start = ((s32[1,1,8,512]{3,1,0,2:T(1,128)}), s32[1,1,8,512]{3,1,0,2:T(1,128)S(1)}, u32[]{:S(2)}, u32[]{:S(2)}) async-start(s32[1,1,8,512]{3,1,0,2:T(1,128)} %copy.25), calls=%async_computation | async-start | bytes 32768 | tf_op jit(solution)/shard_map/all_to_all | solution.py:95
  32.4 3.0 collective-permute-start.7
  36.7 21.9 %scatter_custom_fusion = f32[32768]{0:T(1024)S(1)} fusion(s32[4096]{0:T(1024)S(1)} %bitcast.88, f32[4096]{0:T(1024)S(1)} %bitcast.92, f32[]{:T(128)} %constant.10.clone.1), kind=kCustom, calls=%fused_computation.374 | custom fusion | flops 4096 | bytes 131076 | tf_op jit(solution)/shard_map/scatter-add | solution.py:101
  59.4 3.3 collective-permute-start
  62.8 2.5 collective-permute-start.2
  65.9 3.5 collective-permute-done.2
  70.8 3.0 collective-permute-start.6
  73.9 2.0 copy.29
  75.8 29.5 %scatter_custom_fusion.1 = f32[32768,3]{1,0:T(8,128)} fusion(s32[4096]{0:T(1024)S(1)} %bitcast.89, f32[4096,3]{1,0:T(8,128)} %copy.29, f32[]{:T(128)} %constant.10.clone.1), kind=kCustom, calls=%fused_computation.4 | custom fusion | flops 12288 | bytes 393728 | tf_op jit(solution)/shard_map/scatter-add | solution.py:104
  105.4 10.0 %copy.30 = f32[3,8,16,256]{3,2,1,0:T(8,128)S(1)} copy(f32[3,8,16,256]{0,3,2,1:T(8,128)} %bitcast.64) | data formatting | bytes 786432 | tf_op jit(solution)/shard_map/reshape | solution.py:104
  118.4 1.9 collective-permute-start.12
  120.3 3.9 %collective-permute-start.13 = (f32[3,1,16,256]{3,2,1,0:T(8,128)S(1)}, f32[3,1,16,256]{3,2,1,0:T(8,128)S(1)}, u32[]{:S(2)}, u32[]{:S(2)}) collective-permute-start(f32[3,1,16,256]{3,2,1,0:T(8,128)S(1)} %get-tuple-element.33), channel_id=1, source_target_pairs={{0,8},{8,16},{16,24},{1,9},{9,17},{17,25},{2,10},{10,18},{18,26},{... | collective-permute-start | bytes 147464 | tf_op jit(solution)/shard_map/ppermute | solution.py:19
  125.6 3.0 collective-permute-start.11
  130.0 4.0 %collective-permute-start.15 = (f32[3,10,1,256]{3,2,1,0:T(1,128)S(1)}, f32[3,10,1,256]{3,2,1,0:T(1,128)S(1)}, u32[]{:S(2)}, u32[]{:S(2)}) collective-permute-start(f32[3,10,1,256]{3,2,1,0:T(1,128)S(1)} %get-tuple-element.25), channel_id=1, source_target_pairs={{0,1},{1,2},{2,3},{3,4},{4,5},{5,6},{6,7},{8,9},{9,10},{10,11},{11... | collective-permute-start | bytes 92168 | tf_op jit(solution)/shard_map/ppermute | solution.py:19
  135.8 3.1 collective-permute-start.16
  139.0 2.7 collective-permute-start.17
  141.7 3.8 %collective-permute-done.17 = f32[1,16,256]{2,1,0:T(8,128)S(1)} collective-permute-done((f32[1,16,256]{2,1,0:T(8,128)S(1)}, f32[1,16,256]{2,1,0:T(8,128)S(1)}, u32[]{:S(2)}, u32[]{:S(2)}) %collective-permute-start.17) | collective-permute-done | bytes 16416 | tf_op jit(solution)/shard_map/ppermute | solution.py:19
  146.8 3.0 collective-permute-start.19
  151.1 1.9 collective-permute-start.20
  153.0 3.9 %collective-permute-start.21 = (f32[1,16,256]{2,1,0:T(8,128)S(1)}, f32[1,16,256]{2,1,0:T(8,128)S(1)}, u32[]{:S(2)}, u32[]{:S(2)}) collective-permute-start(f32[1,16,256]{2,1,0:T(8,128)S(1)} %get-tuple-element.77), channel_id=1, source_target_pairs={{0,8},{8,16},{16,24},{1,9},{9,17},{17,25},{2,10},{10,18},{18,26},{... | collective-permute-start | bytes 49160 | tf_op jit(solution)/shard_map/ppermute | solution.py:19
  156.9 2.6 collective-permute-done.21
  160.9 5.2 %collective-permute-start.23 = (f32[10,1,256]{2,1,0:T(1,128)S(1)}, f32[10,1,256]{2,1,0:T(1,128)S(1)}, u32[]{:S(2)}, u32[]{:S(2)}) collective-permute-start(f32[10,1,256]{2,1,0:T(1,128)S(1)} %get-tuple-element.57), channel_id=1, source_target_pairs={{0,1},{1,2},{2,3},{3,4},{4,5},{5,6},{6,7},{8,9},{9,10},{10,11},{11... | collective-permute-start | bytes 30728 | tf_op jit(solution)/shard_map/ppermute | solution.py:19
  167.2 1.9 collective-permute-start.24
  169.1 3.9 %collective-permute-start.25 = (f32[1,16,256]{2,1,0:T(8,128)S(1)}, f32[1,16,256]{2,1,0:T(8,128)S(1)}, u32[]{:S(2)}, u32[]{:S(2)}) collective-permute-start(f32[1,16,256]{2,1,0:T(8,128)S(1)} %get-tuple-element.75), channel_id=1, source_target_pairs={{0,8},{8,16},{16,24},{1,9},{9,17},{17,25},{2,10},{10,18},{18,26},{... | collective-permute-start | bytes 49160 | tf_op jit(solution)/shard_map/ppermute | solution.py:19
  173.0 2.6 collective-permute-done.25
  177.0 4.8 %collective-permute-start.27 = (f32[10,1,256]{2,1,0:T(1,128)S(1)}, f32[10,1,256]{2,1,0:T(1,128)S(1)}, u32[]{:S(2)}, u32[]{:S(2)}) collective-permute-start(f32[10,1,256]{2,1,0:T(1,128)S(1)} %get-tuple-element.55), channel_id=1, source_target_pairs={{0,1},{1,2},{2,3},{3,4},{4,5},{5,6},{6,7},{8,9},{9,10},{10,11},{11... | collective-permute-start | bytes 30728 | tf_op jit(solution)/shard_map/ppermute | solution.py:19
  183.0 1.9 collective-permute-start.28
  184.9 3.9 %collective-permute-start.29 = (f32[1,16,256]{2,1,0:T(8,128)S(1)}, f32[1,16,256]{2,1,0:T(8,128)S(1)}, u32[]{:S(2)}, u32[]{:S(2)}) collective-permute-start(f32[1,16,256]{2,1,0:T(8,128)S(1)} %get-tuple-element.73), channel_id=1, source_target_pairs={{0,8},{8,16},{16,24},{1,9},{9,17},{17,25},{2,10},{10,18},{18,26},{... | collective-permute-start | bytes 49160 | tf_op jit(solution)/shard_map/ppermute | solution.py:19
  188.8 2.6 collective-permute-done.29
  192.8 4.8 %collective-permute-start.31 = (f32[10,1,256]{2,1,0:T(1,128)S(1)}, f32[10,1,256]{2,1,0:T(1,128)S(1)}, u32[]{:S(2)}, u32[]{:S(2)}) collective-permute-start(f32[10,1,256]{2,1,0:T(1,128)S(1)} %get-tuple-element.53), channel_id=1, source_target_pairs={{0,1},{1,2},{2,3},{3,4},{4,5},{5,6},{6,7},{8,9},{9,10},{10,11},{11... | collective-permute-start | bytes 30728 | tf_op jit(solution)/shard_map/ppermute | solution.py:19
  198.9 1.9 collective-permute-start.32
  200.8 3.9 %collective-permute-start.33 = (f32[3,1,16,256]{3,2,1,0:T(8,128)S(1)}, f32[3,1,16,256]{3,2,1,0:T(8,128)S(1)}, u32[]{:S(2)}, u32[]{:S(2)}) collective-permute-start(f32[3,1,16,256]{3,2,1,0:T(8,128)S(1)} %get-tuple-element.31), channel_id=1, source_target_pairs={{0,8},{8,16},{16,24},{1,9},{9,17},{17,25},{2,10},{10,18},{18,26},{... | collective-permute-start | bytes 147464 | tf_op jit(solution)/shard_map/ppermute | solution.py:19
  204.9 2.8 collective-permute-done.33
  209.1 4.8 %collective-permute-start.35 = (f32[3,10,1,256]{3,2,1,0:T(1,128)S(1)}, f32[3,10,1,256]{3,2,1,0:T(1,128)S(1)}, u32[]{:S(2)}, u32[]{:S(2)}) collective-permute-start(f32[3,10,1,256]{3,2,1,0:T(1,128)S(1)} %get-tuple-element.23), channel_id=1, source_target_pairs={{0,1},{1,2},{2,3},{3,4},{4,5},{5,6},{6,7},{8,9},{9,10},{10,11},{11... | collective-permute-start | bytes 92168 | tf_op jit(solution)/shard_map/ppermute | solution.py:19
  215.9 1.9 collective-permute-start.36
  217.8 3.9 %collective-permute-start.37 = (f32[3,1,16,256]{3,2,1,0:T(8,128)S(1)}, f32[3,1,16,256]{3,2,1,0:T(8,128)S(1)}, u32[]{:S(2)}, u32[]{:S(2)}) collective-permute-start(f32[3,1,16,256]{3,2,1,0:T(8,128)S(1)} %get-tuple-element.29), channel_id=1, source_target_pairs={{0,8},{8,16},{16,24},{1,9},{9,17},{17,25},{2,10},{10,18},{18,26},{... | collective-permute-start | bytes 147464 | tf_op jit(solution)/shard_map/ppermute | solution.py:19
  221.9 2.8 collective-permute-done.37
  226.1 5.0 %collective-permute-start.39 = (f32[3,10,1,256]{3,2,1,0:T(1,128)S(1)}, f32[3,10,1,256]{3,2,1,0:T(1,128)S(1)}, u32[]{:S(2)}, u32[]{:S(2)}) collective-permute-start(f32[3,10,1,256]{3,2,1,0:T(1,128)S(1)} %get-tuple-element.21), channel_id=1, source_target_pairs={{0,1},{1,2},{2,3},{3,4},{4,5},{5,6},{6,7},{8,9},{9,10},{10,11},{11... | collective-permute-start | bytes 92168 | tf_op jit(solution)/shard_map/ppermute | solution.py:19
  232.8 1.9 collective-permute-start.40
  234.7 3.9 %collective-permute-start.41 = (f32[1,16,256]{2,1,0:T(8,128)S(1)}, f32[1,16,256]{2,1,0:T(8,128)S(1)}, u32[]{:S(2)}, u32[]{:S(2)}) collective-permute-start(f32[1,16,256]{2,1,0:T(8,128)S(1)} %get-tuple-element.71), channel_id=1, source_target_pairs={{0,8},{8,16},{16,24},{1,9},{9,17},{17,25},{2,10},{10,18},{18,26},{... | collective-permute-start | bytes 49160 | tf_op jit(solution)/shard_map/ppermute | solution.py:19
  238.6 2.6 collective-permute-done.41
  242.6 5.0 %collective-permute-start.43 = (f32[10,1,256]{2,1,0:T(1,128)S(1)}, f32[10,1,256]{2,1,0:T(1,128)S(1)}, u32[]{:S(2)}, u32[]{:S(2)}) collective-permute-start(f32[10,1,256]{2,1,0:T(1,128)S(1)} %get-tuple-element.49), channel_id=1, source_target_pairs={{0,1},{1,2},{2,3},{3,4},{4,5},{5,6},{6,7},{8,9},{9,10},{10,11},{11... | collective-permute-start | bytes 30728 | tf_op jit(solution)/shard_map/ppermute | solution.py:19
  248.8 1.9 collective-permute-start.44
  250.7 3.9 %collective-permute-start.45 = (f32[1,16,256]{2,1,0:T(8,128)S(1)}, f32[1,16,256]{2,1,0:T(8,128)S(1)}, u32[]{:S(2)}, u32[]{:S(2)}) collective-permute-start(f32[1,16,256]{2,1,0:T(8,128)S(1)} %get-tuple-element.69), channel_id=1, source_target_pairs={{0,8},{8,16},{16,24},{1,9},{9,17},{17,25},{2,10},{10,18},{18,26},{... | collective-permute-start | bytes 49160 | tf_op jit(solution)/shard_map/ppermute | solution.py:19
  254.7 2.6 collective-permute-done.45
  258.6 4.8 %collective-permute-start.47 = (f32[10,1,256]{2,1,0:T(1,128)S(1)}, f32[10,1,256]{2,1,0:T(1,128)S(1)}, u32[]{:S(2)}, u32[]{:S(2)}) collective-permute-start(f32[10,1,256]{2,1,0:T(1,128)S(1)} %get-tuple-element.47), channel_id=1, source_target_pairs={{0,1},{1,2},{2,3},{3,4},{4,5},{5,6},{6,7},{8,9},{9,10},{10,11},{11... | collective-permute-start | bytes 30728 | tf_op jit(solution)/shard_map/ppermute | solution.py:19
  264.7 1.9 collective-permute-start.48
  266.6 3.9 %collective-permute-start.49 = (f32[1,16,256]{2,1,0:T(8,128)S(1)}, f32[1,16,256]{2,1,0:T(8,128)S(1)}, u32[]{:S(2)}, u32[]{:S(2)}) collective-permute-start(f32[1,16,256]{2,1,0:T(8,128)S(1)} %get-tuple-element.67), channel_id=1, source_target_pairs={{0,8},{8,16},{16,24},{1,9},{9,17},{17,25},{2,10},{10,18},{18,26},{... | collective-permute-start | bytes 49160 | tf_op jit(solution)/shard_map/ppermute | solution.py:19
  270.5 2.6 collective-permute-done.49
  274.5 4.8 %collective-permute-start.51 = (f32[10,1,256]{2,1,0:T(1,128)S(1)}, f32[10,1,256]{2,1,0:T(1,128)S(1)}, u32[]{:S(2)}, u32[]{:S(2)}) collective-permute-start(f32[10,1,256]{2,1,0:T(1,128)S(1)} %get-tuple-element.45), channel_id=1, source_target_pairs={{0,1},{1,2},{2,3},{3,4},{4,5},{5,6},{6,7},{8,9},{9,10},{10,11},{11... | collective-permute-start | bytes 30728 | tf_op jit(solution)/shard_map/ppermute | solution.py:19
  280.5 1.9 collective-permute-start.52
  282.4 3.9 %collective-permute-start.53 = (f32[1,16,256]{2,1,0:T(8,128)S(1)}, f32[1,16,256]{2,1,0:T(8,128)S(1)}, u32[]{:S(2)}, u32[]{:S(2)}) collective-permute-start(f32[1,16,256]{2,1,0:T(8,128)S(1)} %get-tuple-element.65), channel_id=1, source_target_pairs={{0,8},{8,16},{16,24},{1,9},{9,17},{17,25},{2,10},{10,18},{18,26},{... | collective-permute-start | bytes 49160 | tf_op jit(solution)/shard_map/ppermute | solution.py:19
  286.4 2.6 collective-permute-done.53
  290.3 4.8 %collective-permute-start.55 = (f32[10,1,256]{2,1,0:T(1,128)S(1)}, f32[10,1,256]{2,1,0:T(1,128)S(1)}, u32[]{:S(2)}, u32[]{:S(2)}) collective-permute-start(f32[10,1,256]{2,1,0:T(1,128)S(1)} %get-tuple-element.43), channel_id=1, source_target_pairs={{0,1},{1,2},{2,3},{3,4},{4,5},{5,6},{6,7},{8,9},{9,10},{10,11},{11... | collective-permute-start | bytes 30728 | tf_op jit(solution)/shard_map/ppermute | solution.py:19
  295.1 23.0 %gather_fusion.1 = f32[4096]{0:T(1024)S(1)} fusion(f32[32768]{0:T(1024)S(1)} %subtract_maximum_fusion, s32[4096]{0:T(1024)S(1)} %broadcast_clamp_fusion), kind=kCustom, calls=%fused_computation.1 | custom fusion | bytes 49152 | tf_op jit(solution)/shard_map/gather | solution.py:133
  318.7 8.7 %copy.32 = f32[3,8,16,256]{0,3,2,1:T(8,128)} copy(f32[3,8,16,256]{3,2,1,0:T(8,128)S(1)} %fusion.54) | data formatting | bytes 786432 | tf_op jit(solution)/shard_map/sub | solution.py:126
  327.4 16.5 %gather_fusion = f32[4096,3]{1,0:T(8,128)S(1)} fusion(f32[3,32768]{0,1:T(8,128)} %bitcast.65, s32[4096]{0:T(1024)S(1)} %broadcast_clamp_fusion), kind=kCustom, calls=%fused_computation | custom fusion | bytes 114688 | tf_op jit(solution)/shard_map/gather | solution.py:131
  349.4 7.2 %all-to-all-start.2 = ((f32[8,1,1,1,4,512]{5,4,3,2,1,0:T(4,128)}), f32[8,1,1,1,4,512]{5,4,3,2,1,0:T(4,128)S(1)}, u32[]{:S(2)}, u32[]{:S(2)}) async-start(f32[8,1,1,1,4,512]{5,4,3,2,1,0:T(4,128)} %constant_dynamic-update-slice_fusion.6), calls=%async_computation.2 | async-start | bytes 131072 | tf_op jit(solution)/shard_map/all_to_all | solution.py:136
  356.6 5.9 %all-to-all-done.2 = f32[8,1,1,1,4,512]{5,4,3,2,1,0:T(4,128)S(1)} async-done(((f32[8,1,1,1,4,512]{5,4,3,2,1,0:T(4,128)}), f32[8,1,1,1,4,512]{5,4,3,2,1,0:T(4,128)S(1)}, u32[]{:S(2)}, u32[]{:S(2)}) %all-to-all-start.2) | async-done | bytes 65568 | tf_op jit(solution)/shard_map/all_to_all | solution.py:136
  (200 shorter events, 52.5 us)
Async XLA Ops:
  0.6 25.2 %copy-start.1 = (f32[3,8,16,256]{3,2,1,0:T(8,128)S(1)}, f32[3,8,16,256]{3,2,1,0:T(8,128)}, u32[]{:S(2)}) copy-start(f32[3,8,16,256]{3,2,1,0:T(8,128)} %param.6) | copy-start | bytes 1179652
  3.6 22.3 %all-to-all-start.1 = ((f32[1,1,8,4,512]{4,3,1,0,2:T(4,128)}), f32[1,1,8,4,512]{4,3,1,0,2:T(4,128)S(1)}, u32[]{:S(2)}, u32[]{:S(2)}) async-start(f32[1,1,8,4,512]{4,3,1,0,2:T(4,128)} %pad_maximum_fusion.104), calls=%async_computation.1 | async-start | bytes 131072 | tf_op jit(solution)/shard_map/all_to_all | solution.py:96
  9.2 14.8 %collective-permute-start.9 = (f32[1,16,256]{2,1,0:T(8,128)S(1)}, f32[1,16,256]{2,1,0:T(8,128)S(1)}, u32[]{:S(2)}, u32[]{:S(2)}) collective-permute-start(f32[1,16,256]{2,1,0:T(8,128)S(1)} %get-tuple-element.82), channel_id=1, source_target_pairs={{0,8},{8,16},{16,24},{1,9},{9,17},{17,25},{2,10},{10,18},{18,26},{... | collective-permute-start | bytes 49160 | tf_op jit(solution)/shard_map/ppermute | solution.py:19
  13.4 12.4 %collective-permute-start.3 = (f32[3,1,16,256]{3,2,1,0:T(8,128)S(1)}, f32[3,1,16,256]{3,2,1,0:T(8,128)S(1)}, u32[]{:S(2)}, u32[]{:S(2)}) collective-permute-start(f32[3,1,16,256]{3,2,1,0:T(8,128)S(1)} %get-tuple-element.36), channel_id=1, source_target_pairs={{0,8},{8,16},{16,24},{1,9},{9,17},{17,25},{2,10},{10,18},{18,26},{... | collective-permute-start | bytes 147464 | tf_op jit(solution)/shard_map/ppermute | solution.py:19
  15.4 10.5 %collective-permute-start.1 = (f32[3,1,16,256]{3,2,1,0:T(8,128)S(1)}, f32[3,1,16,256]{3,2,1,0:T(8,128)S(1)}, u32[]{:S(2)}, u32[]{:S(2)}) collective-permute-start(f32[3,1,16,256]{3,2,1,0:T(8,128)S(1)} %get-tuple-element.35), channel_id=1, source_target_pairs={{8,0},{16,8},{24,16},{9,1},{17,9},{25,17},{10,2},{18,10},{26,18},{... | collective-permute-start | bytes 147464 | tf_op jit(solution)/shard_map/ppermute | solution.py:22
  20.2 5.6 %collective-permute-start.8 = (f32[1,16,256]{2,1,0:T(8,128)S(1)}, f32[1,16,256]{2,1,0:T(8,128)S(1)}, u32[]{:S(2)}, u32[]{:S(2)}) collective-permute-start(f32[1,16,256]{2,1,0:T(8,128)S(1)} %get-tuple-element.81), channel_id=1, source_target_pairs={{8,0},{16,8},{24,16},{9,1},{17,9},{25,17},{10,2},{18,10},{26,18},{... | collective-permute-start | bytes 49160 | tf_op jit(solution)/shard_map/ppermute | solution.py:22
  25.8 40.1 %copy-start.5 = (f32[10,16,256]{2,1,0:T(8,128)}, f32[10,16,256]{2,1,0:T(8,128)S(1)}, u32[]{:S(2)}) copy-start(f32[10,16,256]{2,1,0:T(8,128)S(1)} %constant_dynamic-update-slice_fusion.3) | copy-start | bytes 491524
  25.9 33.5 %copy-start.8 = (f32[3,1,16,256]{3,2,1,0:T(8,128)}, f32[3,1,16,256]{3,2,1,0:T(8,128)S(1)}, u32[]{:S(2)}) copy-start(f32[3,1,16,256]{3,2,1,0:T(8,128)S(1)} %collective-permute-done.1) | copy-start | bytes 147460
  25.9 10.8 %all-to-all-start = ((s32[1,1,8,512]{3,1,0,2:T(1,128)}), s32[1,1,8,512]{3,1,0,2:T(1,128)S(1)}, u32[]{:S(2)}, u32[]{:S(2)}) async-start(s32[1,1,8,512]{3,1,0,2:T(1,128)} %copy.25), calls=%async_computation | async-start | bytes 32768 | tf_op jit(solution)/shard_map/all_to_all | solution.py:95
  31.1 34.2 %collective-permute-start.5 = (f32[3,10,1,256]{3,2,1,0:T(1,128)S(1)}, f32[3,10,1,256]{3,2,1,0:T(1,128)S(1)}, u32[]{:S(2)}, u32[]{:S(2)}) collective-permute-start(f32[3,10,1,256]{3,2,1,0:T(1,128)S(1)} %get-tuple-element.28), channel_id=1, source_target_pairs={{1,0},{2,1},{3,2},{4,3},{5,4},{6,5},{7,6},{9,8},{10,9},{11,10},{12... | collective-permute-start | bytes 92168 | tf_op jit(solution)/shard_map/ppermute | solution.py:22
  32.4 32.9 %collective-permute-start.7 = (f32[3,10,1,256]{3,2,1,0:T(1,128)S(1)}, f32[3,10,1,256]{3,2,1,0:T(1,128)S(1)}, u32[]{:S(2)}, u32[]{:S(2)}) collective-permute-start(f32[3,10,1,256]{3,2,1,0:T(1,128)S(1)} %get-tuple-element.27), channel_id=1, source_target_pairs={{0,1},{1,2},{2,3},{3,4},{4,5},{5,6},{6,7},{8,9},{9,10},{10,11},{11... | collective-permute-start | bytes 92168 | tf_op jit(solution)/shard_map/ppermute | solution.py:19
  36.7 39.1 %copy-start.22 = (s32[1,1,8,512]{3,1,0,2:T(1,128)}, s32[1,1,8,512]{3,1,0,2:T(1,128)S(1)}, u32[]{:S(2)}) copy-start(s32[1,1,8,512]{3,1,0,2:T(1,128)S(1)} %all-to-all-done) | copy-start | bytes 49156
  59.4 6.5 %collective-permute-start = (f32[2,16,256]{2,1,0:T(8,128)S(1)}, f32[2,16,256]{2,1,0:T(8,128)S(1)}, u32[]{:S(2)}, u32[]{:S(2)}) collective-permute-start(f32[2,16,256]{2,1,0:T(8,128)S(1)} %get-tuple-element.84), channel_id=1, source_target_pairs={{8,0},{16,8},{24,16},{9,1},{17,9},{25,17},{10,2},{18,10},{26,18},{... | collective-permute-start | bytes 98312 | tf_op jit(solution)/shard_map/ppermute | solution.py:22
  62.8 6.7 %collective-permute-start.2 = (f32[2,16,256]{2,1,0:T(8,128)S(1)}, f32[2,16,256]{2,1,0:T(8,128)S(1)}, u32[]{:S(2)}, u32[]{:S(2)}) collective-permute-start(f32[2,16,256]{2,1,0:T(8,128)S(1)} %get-tuple-element.83), channel_id=1, source_target_pairs={{0,8},{8,16},{16,24},{1,9},{9,17},{17,25},{2,10},{10,18},{18,26},{... | collective-permute-start | bytes 98312 | tf_op jit(solution)/shard_map/ppermute | solution.py:19
  69.5 45.9 %collective-permute-start.4 = (f32[12,2,256]{2,1,0:T(2,128)S(1)}, f32[12,2,256]{2,1,0:T(2,128)S(1)}, u32[]{:S(2)}, u32[]{:S(2)}) collective-permute-start(f32[12,2,256]{2,1,0:T(2,128)S(1)} %get-tuple-element.40), channel_id=1, source_target_pairs={{1,0},{2,1},{3,2},{4,3},{5,4},{6,5},{7,6},{9,8},{10,9},{11,10},{12... | collective-permute-start | bytes 73736 | tf_op jit(solution)/shard_map/ppermute | solution.py:22
  70.8 44.6 %collective-permute-start.6 = (f32[12,2,256]{2,1,0:T(2,128)S(1)}, f32[12,2,256]{2,1,0:T(2,128)S(1)}, u32[]{:S(2)}, u32[]{:S(2)}) collective-permute-start(f32[12,2,256]{2,1,0:T(2,128)S(1)} %get-tuple-element.39), channel_id=1, source_target_pairs={{0,1},{1,2},{2,3},{3,4},{4,5},{5,6},{6,7},{8,9},{9,10},{10,11},{11... | collective-permute-start | bytes 73736 | tf_op jit(solution)/shard_map/ppermute | solution.py:19
  118.4 10.2 %collective-permute-start.12 = (f32[3,1,16,256]{3,2,1,0:T(8,128)S(1)}, f32[3,1,16,256]{3,2,1,0:T(8,128)S(1)}, u32[]{:S(2)}, u32[]{:S(2)}) collective-permute-start(f32[3,1,16,256]{3,2,1,0:T(8,128)S(1)} %get-tuple-element.34), channel_id=1, source_target_pairs={{8,0},{16,8},{24,16},{9,1},{17,9},{25,17},{10,2},{18,10},{26,18},{... | collective-permute-start | bytes 147464 | tf_op jit(solution)/shard_map/ppermute | solution.py:22
  120.3 8.3 %collective-permute-start.13 = (f32[3,1,16,256]{3,2,1,0:T(8,128)S(1)}, f32[3,1,16,256]{3,2,1,0:T(8,128)S(1)}, u32[]{:S(2)}, u32[]{:S(2)}) collective-permute-start(f32[3,1,16,256]{3,2,1,0:T(8,128)S(1)} %get-tuple-element.33), channel_id=1, source_target_pairs={{0,8},{8,16},{16,24},{1,9},{9,17},{17,25},{2,10},{10,18},{18,26},{... | collective-permute-start | bytes 147464 | tf_op jit(solution)/shard_map/ppermute | solution.py:19
  124.3 9.8 %collective-permute-start.10 = (f32[10,1,256]{2,1,0:T(1,128)S(1)}, f32[10,1,256]{2,1,0:T(1,128)S(1)}, u32[]{:S(2)}, u32[]{:S(2)}) collective-permute-start(f32[10,1,256]{2,1,0:T(1,128)S(1)} %get-tuple-element.62), channel_id=1, source_target_pairs={{1,0},{2,1},{3,2},{4,3},{5,4},{6,5},{7,6},{9,8},{10,9},{11,10},{12... | collective-permute-start | bytes 30728 | tf_op jit(solution)/shard_map/ppermute | solution.py:22
  125.6 8.5 %collective-permute-start.11 = (f32[10,1,256]{2,1,0:T(1,128)S(1)}, f32[10,1,256]{2,1,0:T(1,128)S(1)}, u32[]{:S(2)}, u32[]{:S(2)}) collective-permute-start(f32[10,1,256]{2,1,0:T(1,128)S(1)} %get-tuple-element.61), channel_id=1, source_target_pairs={{0,1},{1,2},{2,3},{3,4},{4,5},{5,6},{6,7},{8,9},{9,10},{10,11},{11... | collective-permute-start | bytes 30728 | tf_op jit(solution)/shard_map/ppermute | solution.py:19
  128.7 5.6 %collective-permute-start.14 = (f32[3,10,1,256]{3,2,1,0:T(1,128)S(1)}, f32[3,10,1,256]{3,2,1,0:T(1,128)S(1)}, u32[]{:S(2)}, u32[]{:S(2)}) collective-permute-start(f32[3,10,1,256]{3,2,1,0:T(1,128)S(1)} %get-tuple-element.26), channel_id=1, source_target_pairs={{1,0},{2,1},{3,2},{4,3},{5,4},{6,5},{7,6},{9,8},{10,9},{11,10},{12... | collective-permute-start | bytes 92168 | tf_op jit(solution)/shard_map/ppermute | solution.py:22
  130.0 4.9 %collective-permute-start.15 = (f32[3,10,1,256]{3,2,1,0:T(1,128)S(1)}, f32[3,10,1,256]{3,2,1,0:T(1,128)S(1)}, u32[]{:S(2)}, u32[]{:S(2)}) collective-permute-start(f32[3,10,1,256]{3,2,1,0:T(1,128)S(1)} %get-tuple-element.25), channel_id=1, source_target_pairs={{0,1},{1,2},{2,3},{3,4},{4,5},{5,6},{6,7},{8,9},{9,10},{10,11},{11... | collective-permute-start | bytes 92168 | tf_op jit(solution)/shard_map/ppermute | solution.py:19
  135.8 5.9 %collective-permute-start.16 = (f32[1,16,256]{2,1,0:T(8,128)S(1)}, f32[1,16,256]{2,1,0:T(8,128)S(1)}, u32[]{:S(2)}, u32[]{:S(2)}) collective-permute-start(f32[1,16,256]{2,1,0:T(8,128)S(1)} %get-tuple-element.80), channel_id=1, source_target_pairs={{8,0},{16,8},{24,16},{9,1},{17,9},{25,17},{10,2},{18,10},{26,18},{... | collective-permute-start | bytes 49160 | tf_op jit(solution)/shard_map/ppermute | solution.py:22
  139.0 6.5 %collective-permute-start.17 = (f32[1,16,256]{2,1,0:T(8,128)S(1)}, f32[1,16,256]{2,1,0:T(8,128)S(1)}, u32[]{:S(2)}, u32[]{:S(2)}) collective-permute-start(f32[1,16,256]{2,1,0:T(8,128)S(1)} %get-tuple-element.79), channel_id=1, source_target_pairs={{0,8},{8,16},{16,24},{1,9},{9,17},{17,25},{2,10},{10,18},{18,26},{... | collective-permute-start | bytes 49160 | tf_op jit(solution)/shard_map/ppermute | solution.py:19
  145.5 4.3 %collective-permute-start.18 = (f32[10,1,256]{2,1,0:T(1,128)S(1)}, f32[10,1,256]{2,1,0:T(1,128)S(1)}, u32[]{:S(2)}, u32[]{:S(2)}) collective-permute-start(f32[10,1,256]{2,1,0:T(1,128)S(1)} %get-tuple-element.60), channel_id=1, source_target_pairs={{1,0},{2,1},{3,2},{4,3},{5,4},{6,5},{7,6},{9,8},{10,9},{11,10},{12... | collective-permute-start | bytes 30728 | tf_op jit(solution)/shard_map/ppermute | solution.py:22
  146.8 3.9 %collective-permute-start.19 = (f32[10,1,256]{2,1,0:T(1,128)S(1)}, f32[10,1,256]{2,1,0:T(1,128)S(1)}, u32[]{:S(2)}, u32[]{:S(2)}) collective-permute-start(f32[10,1,256]{2,1,0:T(1,128)S(1)} %get-tuple-element.59), channel_id=1, source_target_pairs={{0,1},{1,2},{2,3},{3,4},{4,5},{5,6},{6,7},{8,9},{9,10},{10,11},{11... | collective-permute-start | bytes 30728 | tf_op jit(solution)/shard_map/ppermute | solution.py:19
  151.1 5.9 %collective-permute-start.20 = (f32[1,16,256]{2,1,0:T(8,128)S(1)}, f32[1,16,256]{2,1,0:T(8,128)S(1)}, u32[]{:S(2)}, u32[]{:S(2)}) collective-permute-start(f32[1,16,256]{2,1,0:T(8,128)S(1)} %get-tuple-element.78), channel_id=1, source_target_pairs={{8,0},{16,8},{24,16},{9,1},{17,9},{25,17},{10,2},{18,10},{26,18},{... | collective-permute-start | bytes 49160 | tf_op jit(solution)/shard_map/ppermute | solution.py:22
  153.0 6.5 %collective-permute-start.21 = (f32[1,16,256]{2,1,0:T(8,128)S(1)}, f32[1,16,256]{2,1,0:T(8,128)S(1)}, u32[]{:S(2)}, u32[]{:S(2)}) collective-permute-start(f32[1,16,256]{2,1,0:T(8,128)S(1)} %get-tuple-element.77), channel_id=1, source_target_pairs={{0,8},{8,16},{16,24},{1,9},{9,17},{17,25},{2,10},{10,18},{18,26},{... | collective-permute-start | bytes 49160 | tf_op jit(solution)/shard_map/ppermute | solution.py:19
  159.6 6.6 %collective-permute-start.22 = (f32[10,1,256]{2,1,0:T(1,128)S(1)}, f32[10,1,256]{2,1,0:T(1,128)S(1)}, u32[]{:S(2)}, u32[]{:S(2)}) collective-permute-start(f32[10,1,256]{2,1,0:T(1,128)S(1)} %get-tuple-element.58), channel_id=1, source_target_pairs={{1,0},{2,1},{3,2},{4,3},{5,4},{6,5},{7,6},{9,8},{10,9},{11,10},{12... | collective-permute-start | bytes 30728 | tf_op jit(solution)/shard_map/ppermute | solution.py:22
  160.9 5.9 %collective-permute-start.23 = (f32[10,1,256]{2,1,0:T(1,128)S(1)}, f32[10,1,256]{2,1,0:T(1,128)S(1)}, u32[]{:S(2)}, u32[]{:S(2)}) collective-permute-start(f32[10,1,256]{2,1,0:T(1,128)S(1)} %get-tuple-element.57), channel_id=1, source_target_pairs={{0,1},{1,2},{2,3},{3,4},{4,5},{5,6},{6,7},{8,9},{9,10},{10,11},{11... | collective-permute-start | bytes 30728 | tf_op jit(solution)/shard_map/ppermute | solution.py:19
  167.2 5.9 %collective-permute-start.24 = (f32[1,16,256]{2,1,0:T(8,128)S(1)}, f32[1,16,256]{2,1,0:T(8,128)S(1)}, u32[]{:S(2)}, u32[]{:S(2)}) collective-permute-start(f32[1,16,256]{2,1,0:T(8,128)S(1)} %get-tuple-element.76), channel_id=1, source_target_pairs={{8,0},{16,8},{24,16},{9,1},{17,9},{25,17},{10,2},{18,10},{26,18},{... | collective-permute-start | bytes 49160 | tf_op jit(solution)/shard_map/ppermute | solution.py:22
  169.1 6.5 %collective-permute-start.25 = (f32[1,16,256]{2,1,0:T(8,128)S(1)}, f32[1,16,256]{2,1,0:T(8,128)S(1)}, u32[]{:S(2)}, u32[]{:S(2)}) collective-permute-start(f32[1,16,256]{2,1,0:T(8,128)S(1)} %get-tuple-element.75), channel_id=1, source_target_pairs={{0,8},{8,16},{16,24},{1,9},{9,17},{17,25},{2,10},{10,18},{18,26},{... | collective-permute-start | bytes 49160 | tf_op jit(solution)/shard_map/ppermute | solution.py:19
  175.7 6.1 %collective-permute-start.26 = (f32[10,1,256]{2,1,0:T(1,128)S(1)}, f32[10,1,256]{2,1,0:T(1,128)S(1)}, u32[]{:S(2)}, u32[]{:S(2)}) collective-permute-start(f32[10,1,256]{2,1,0:T(1,128)S(1)} %get-tuple-element.56), channel_id=1, source_target_pairs={{1,0},{2,1},{3,2},{4,3},{5,4},{6,5},{7,6},{9,8},{10,9},{11,10},{12... | collective-permute-start | bytes 30728 | tf_op jit(solution)/shard_map/ppermute | solution.py:22
  177.0 5.6 %collective-permute-start.27 = (f32[10,1,256]{2,1,0:T(1,128)S(1)}, f32[10,1,256]{2,1,0:T(1,128)S(1)}, u32[]{:S(2)}, u32[]{:S(2)}) collective-permute-start(f32[10,1,256]{2,1,0:T(1,128)S(1)} %get-tuple-element.55), channel_id=1, source_target_pairs={{0,1},{1,2},{2,3},{3,4},{4,5},{5,6},{6,7},{8,9},{9,10},{10,11},{11... | collective-permute-start | bytes 30728 | tf_op jit(solution)/shard_map/ppermute | solution.py:19
  183.0 5.9 %collective-permute-start.28 = (f32[1,16,256]{2,1,0:T(8,128)S(1)}, f32[1,16,256]{2,1,0:T(8,128)S(1)}, u32[]{:S(2)}, u32[]{:S(2)}) collective-permute-start(f32[1,16,256]{2,1,0:T(8,128)S(1)} %get-tuple-element.74), channel_id=1, source_target_pairs={{8,0},{16,8},{24,16},{9,1},{17,9},{25,17},{10,2},{18,10},{26,18},{... | collective-permute-start | bytes 49160 | tf_op jit(solution)/shard_map/ppermute | solution.py:22
  184.9 6.5 %collective-permute-start.29 = (f32[1,16,256]{2,1,0:T(8,128)S(1)}, f32[1,16,256]{2,1,0:T(8,128)S(1)}, u32[]{:S(2)}, u32[]{:S(2)}) collective-permute-start(f32[1,16,256]{2,1,0:T(8,128)S(1)} %get-tuple-element.73), channel_id=1, source_target_pairs={{0,8},{8,16},{16,24},{1,9},{9,17},{17,25},{2,10},{10,18},{18,26},{... | collective-permute-start | bytes 49160 | tf_op jit(solution)/shard_map/ppermute | solution.py:19
  191.5 6.1 %collective-permute-start.30 = (f32[10,1,256]{2,1,0:T(1,128)S(1)}, f32[10,1,256]{2,1,0:T(1,128)S(1)}, u32[]{:S(2)}, u32[]{:S(2)}) collective-permute-start(f32[10,1,256]{2,1,0:T(1,128)S(1)} %get-tuple-element.54), channel_id=1, source_target_pairs={{1,0},{2,1},{3,2},{4,3},{5,4},{6,5},{7,6},{9,8},{10,9},{11,10},{12... | collective-permute-start | bytes 30728 | tf_op jit(solution)/shard_map/ppermute | solution.py:22
  192.8 5.6 %collective-permute-start.31 = (f32[10,1,256]{2,1,0:T(1,128)S(1)}, f32[10,1,256]{2,1,0:T(1,128)S(1)}, u32[]{:S(2)}, u32[]{:S(2)}) collective-permute-start(f32[10,1,256]{2,1,0:T(1,128)S(1)} %get-tuple-element.53), channel_id=1, source_target_pairs={{0,1},{1,2},{2,3},{3,4},{4,5},{5,6},{6,7},{8,9},{9,10},{10,11},{11... | collective-permute-start | bytes 30728 | tf_op jit(solution)/shard_map/ppermute | solution.py:19
  198.9 6.0 %collective-permute-start.32 = (f32[3,1,16,256]{3,2,1,0:T(8,128)S(1)}, f32[3,1,16,256]{3,2,1,0:T(8,128)S(1)}, u32[]{:S(2)}, u32[]{:S(2)}) collective-permute-start(f32[3,1,16,256]{3,2,1,0:T(8,128)S(1)} %get-tuple-element.32), channel_id=1, source_target_pairs={{8,0},{16,8},{24,16},{9,1},{17,9},{25,17},{10,2},{18,10},{26,18},{... | collective-permute-start | bytes 147464 | tf_op jit(solution)/shard_map/ppermute | solution.py:22
  200.8 6.9 %collective-permute-start.33 = (f32[3,1,16,256]{3,2,1,0:T(8,128)S(1)}, f32[3,1,16,256]{3,2,1,0:T(8,128)S(1)}, u32[]{:S(2)}, u32[]{:S(2)}) collective-permute-start(f32[3,1,16,256]{3,2,1,0:T(8,128)S(1)} %get-tuple-element.31), channel_id=1, source_target_pairs={{0,8},{8,16},{16,24},{1,9},{9,17},{17,25},{2,10},{10,18},{18,26},{... | collective-permute-start | bytes 147464 | tf_op jit(solution)/shard_map/ppermute | solution.py:19
  207.8 6.1 %collective-permute-start.34 = (f32[3,10,1,256]{3,2,1,0:T(1,128)S(1)}, f32[3,10,1,256]{3,2,1,0:T(1,128)S(1)}, u32[]{:S(2)}, u32[]{:S(2)}) collective-permute-start(f32[3,10,1,256]{3,2,1,0:T(1,128)S(1)} %get-tuple-element.24), channel_id=1, source_target_pairs={{1,0},{2,1},{3,2},{4,3},{5,4},{6,5},{7,6},{9,8},{10,9},{11,10},{12... | collective-permute-start | bytes 92168 | tf_op jit(solution)/shard_map/ppermute | solution.py:22
  209.1 5.6 %collective-permute-start.35 = (f32[3,10,1,256]{3,2,1,0:T(1,128)S(1)}, f32[3,10,1,256]{3,2,1,0:T(1,128)S(1)}, u32[]{:S(2)}, u32[]{:S(2)}) collective-permute-start(f32[3,10,1,256]{3,2,1,0:T(1,128)S(1)} %get-tuple-element.23), channel_id=1, source_target_pairs={{0,1},{1,2},{2,3},{3,4},{4,5},{5,6},{6,7},{8,9},{9,10},{10,11},{11... | collective-permute-start | bytes 92168 | tf_op jit(solution)/shard_map/ppermute | solution.py:19
  215.9 6.0 %collective-permute-start.36 = (f32[3,1,16,256]{3,2,1,0:T(8,128)S(1)}, f32[3,1,16,256]{3,2,1,0:T(8,128)S(1)}, u32[]{:S(2)}, u32[]{:S(2)}) collective-permute-start(f32[3,1,16,256]{3,2,1,0:T(8,128)S(1)} %get-tuple-element.30), channel_id=1, source_target_pairs={{8,0},{16,8},{24,16},{9,1},{17,9},{25,17},{10,2},{18,10},{26,18},{... | collective-permute-start | bytes 147464 | tf_op jit(solution)/shard_map/ppermute | solution.py:22
  217.8 6.9 %collective-permute-start.37 = (f32[3,1,16,256]{3,2,1,0:T(8,128)S(1)}, f32[3,1,16,256]{3,2,1,0:T(8,128)S(1)}, u32[]{:S(2)}, u32[]{:S(2)}) collective-permute-start(f32[3,1,16,256]{3,2,1,0:T(8,128)S(1)} %get-tuple-element.29), channel_id=1, source_target_pairs={{0,8},{8,16},{16,24},{1,9},{9,17},{17,25},{2,10},{10,18},{18,26},{... | collective-permute-start | bytes 147464 | tf_op jit(solution)/shard_map/ppermute | solution.py:19
  224.8 6.3 %collective-permute-start.38 = (f32[3,10,1,256]{3,2,1,0:T(1,128)S(1)}, f32[3,10,1,256]{3,2,1,0:T(1,128)S(1)}, u32[]{:S(2)}, u32[]{:S(2)}) collective-permute-start(f32[3,10,1,256]{3,2,1,0:T(1,128)S(1)} %get-tuple-element.22), channel_id=1, source_target_pairs={{1,0},{2,1},{3,2},{4,3},{5,4},{6,5},{7,6},{9,8},{10,9},{11,10},{12... | collective-permute-start | bytes 92168 | tf_op jit(solution)/shard_map/ppermute | solution.py:22
  226.1 5.8 %collective-permute-start.39 = (f32[3,10,1,256]{3,2,1,0:T(1,128)S(1)}, f32[3,10,1,256]{3,2,1,0:T(1,128)S(1)}, u32[]{:S(2)}, u32[]{:S(2)}) collective-permute-start(f32[3,10,1,256]{3,2,1,0:T(1,128)S(1)} %get-tuple-element.21), channel_id=1, source_target_pairs={{0,1},{1,2},{2,3},{3,4},{4,5},{5,6},{6,7},{8,9},{9,10},{10,11},{11... | collective-permute-start | bytes 92168 | tf_op jit(solution)/shard_map/ppermute | solution.py:19
  232.8 5.9 %collective-permute-start.40 = (f32[1,16,256]{2,1,0:T(8,128)S(1)}, f32[1,16,256]{2,1,0:T(8,128)S(1)}, u32[]{:S(2)}, u32[]{:S(2)}) collective-permute-start(f32[1,16,256]{2,1,0:T(8,128)S(1)} %get-tuple-element.72), channel_id=1, source_target_pairs={{8,0},{16,8},{24,16},{9,1},{17,9},{25,17},{10,2},{18,10},{26,18},{... | collective-permute-start | bytes 49160 | tf_op jit(solution)/shard_map/ppermute | solution.py:22
  234.7 6.5 %collective-permute-start.41 = (f32[1,16,256]{2,1,0:T(8,128)S(1)}, f32[1,16,256]{2,1,0:T(8,128)S(1)}, u32[]{:S(2)}, u32[]{:S(2)}) collective-permute-start(f32[1,16,256]{2,1,0:T(8,128)S(1)} %get-tuple-element.71), channel_id=1, source_target_pairs={{0,8},{8,16},{16,24},{1,9},{9,17},{17,25},{2,10},{10,18},{18,26},{... | collective-permute-start | bytes 49160 | tf_op jit(solution)/shard_map/ppermute | solution.py:19
  241.3 6.3 %collective-permute-start.42 = (f32[10,1,256]{2,1,0:T(1,128)S(1)}, f32[10,1,256]{2,1,0:T(1,128)S(1)}, u32[]{:S(2)}, u32[]{:S(2)}) collective-permute-start(f32[10,1,256]{2,1,0:T(1,128)S(1)} %get-tuple-element.50), channel_id=1, source_target_pairs={{1,0},{2,1},{3,2},{4,3},{5,4},{6,5},{7,6},{9,8},{10,9},{11,10},{12... | collective-permute-start | bytes 30728 | tf_op jit(solution)/shard_map/ppermute | solution.py:22
  242.6 5.8 %collective-permute-start.43 = (f32[10,1,256]{2,1,0:T(1,128)S(1)}, f32[10,1,256]{2,1,0:T(1,128)S(1)}, u32[]{:S(2)}, u32[]{:S(2)}) collective-permute-start(f32[10,1,256]{2,1,0:T(1,128)S(1)} %get-tuple-element.49), channel_id=1, source_target_pairs={{0,1},{1,2},{2,3},{3,4},{4,5},{5,6},{6,7},{8,9},{9,10},{10,11},{11... | collective-permute-start | bytes 30728 | tf_op jit(solution)/shard_map/ppermute | solution.py:19
  248.8 5.9 %collective-permute-start.44 = (f32[1,16,256]{2,1,0:T(8,128)S(1)}, f32[1,16,256]{2,1,0:T(8,128)S(1)}, u32[]{:S(2)}, u32[]{:S(2)}) collective-permute-start(f32[1,16,256]{2,1,0:T(8,128)S(1)} %get-tuple-element.70), channel_id=1, source_target_pairs={{8,0},{16,8},{24,16},{9,1},{17,9},{25,17},{10,2},{18,10},{26,18},{... | collective-permute-start | bytes 49160 | tf_op jit(solution)/shard_map/ppermute | solution.py:22
  250.7 6.5 %collective-permute-start.45 = (f32[1,16,256]{2,1,0:T(8,128)S(1)}, f32[1,16,256]{2,1,0:T(8,128)S(1)}, u32[]{:S(2)}, u32[]{:S(2)}) collective-permute-start(f32[1,16,256]{2,1,0:T(8,128)S(1)} %get-tuple-element.69), channel_id=1, source_target_pairs={{0,8},{8,16},{16,24},{1,9},{9,17},{17,25},{2,10},{10,18},{18,26},{... | collective-permute-start | bytes 49160 | tf_op jit(solution)/shard_map/ppermute | solution.py:19
  257.3 6.1 %collective-permute-start.46 = (f32[10,1,256]{2,1,0:T(1,128)S(1)}, f32[10,1,256]{2,1,0:T(1,128)S(1)}, u32[]{:S(2)}, u32[]{:S(2)}) collective-permute-start(f32[10,1,256]{2,1,0:T(1,128)S(1)} %get-tuple-element.48), channel_id=1, source_target_pairs={{1,0},{2,1},{3,2},{4,3},{5,4},{6,5},{7,6},{9,8},{10,9},{11,10},{12... | collective-permute-start | bytes 30728 | tf_op jit(solution)/shard_map/ppermute | solution.py:22
  258.6 5.6 %collective-permute-start.47 = (f32[10,1,256]{2,1,0:T(1,128)S(1)}, f32[10,1,256]{2,1,0:T(1,128)S(1)}, u32[]{:S(2)}, u32[]{:S(2)}) collective-permute-start(f32[10,1,256]{2,1,0:T(1,128)S(1)} %get-tuple-element.47), channel_id=1, source_target_pairs={{0,1},{1,2},{2,3},{3,4},{4,5},{5,6},{6,7},{8,9},{9,10},{10,11},{11... | collective-permute-start | bytes 30728 | tf_op jit(solution)/shard_map/ppermute | solution.py:19
  264.7 5.9 %collective-permute-start.48 = (f32[1,16,256]{2,1,0:T(8,128)S(1)}, f32[1,16,256]{2,1,0:T(8,128)S(1)}, u32[]{:S(2)}, u32[]{:S(2)}) collective-permute-start(f32[1,16,256]{2,1,0:T(8,128)S(1)} %get-tuple-element.68), channel_id=1, source_target_pairs={{8,0},{16,8},{24,16},{9,1},{17,9},{25,17},{10,2},{18,10},{26,18},{... | collective-permute-start | bytes 49160 | tf_op jit(solution)/shard_map/ppermute | solution.py:22
  266.6 6.5 %collective-permute-start.49 = (f32[1,16,256]{2,1,0:T(8,128)S(1)}, f32[1,16,256]{2,1,0:T(8,128)S(1)}, u32[]{:S(2)}, u32[]{:S(2)}) collective-permute-start(f32[1,16,256]{2,1,0:T(8,128)S(1)} %get-tuple-element.67), channel_id=1, source_target_pairs={{0,8},{8,16},{16,24},{1,9},{9,17},{17,25},{2,10},{10,18},{18,26},{... | collective-permute-start | bytes 49160 | tf_op jit(solution)/shard_map/ppermute | solution.py:19
  273.2 6.1 %collective-permute-start.50 = (f32[10,1,256]{2,1,0:T(1,128)S(1)}, f32[10,1,256]{2,1,0:T(1,128)S(1)}, u32[]{:S(2)}, u32[]{:S(2)}) collective-permute-start(f32[10,1,256]{2,1,0:T(1,128)S(1)} %get-tuple-element.46), channel_id=1, source_target_pairs={{1,0},{2,1},{3,2},{4,3},{5,4},{6,5},{7,6},{9,8},{10,9},{11,10},{12... | collective-permute-start | bytes 30728 | tf_op jit(solution)/shard_map/ppermute | solution.py:22
  274.5 5.6 %collective-permute-start.51 = (f32[10,1,256]{2,1,0:T(1,128)S(1)}, f32[10,1,256]{2,1,0:T(1,128)S(1)}, u32[]{:S(2)}, u32[]{:S(2)}) collective-permute-start(f32[10,1,256]{2,1,0:T(1,128)S(1)} %get-tuple-element.45), channel_id=1, source_target_pairs={{0,1},{1,2},{2,3},{3,4},{4,5},{5,6},{6,7},{8,9},{9,10},{10,11},{11... | collective-permute-start | bytes 30728 | tf_op jit(solution)/shard_map/ppermute | solution.py:19
  280.5 38.1 %copy-start = (f32[8,16,256]{2,1,0:T(8,128)}, f32[8,16,256]{2,1,0:T(8,128)S(1)}, u32[]{:S(2)}) copy-start(f32[8,16,256]{2,1,0:T(8,128)S(1)} %fusion.66) | copy-start | bytes 393220
  280.5 5.9 %collective-permute-start.52 = (f32[1,16,256]{2,1,0:T(8,128)S(1)}, f32[1,16,256]{2,1,0:T(8,128)S(1)}, u32[]{:S(2)}, u32[]{:S(2)}) collective-permute-start(f32[1,16,256]{2,1,0:T(8,128)S(1)} %get-tuple-element.66), channel_id=1, source_target_pairs={{8,0},{16,8},{24,16},{9,1},{17,9},{25,17},{10,2},{18,10},{26,18},{... | collective-permute-start | bytes 49160 | tf_op jit(solution)/shard_map/ppermute | solution.py:22
  282.4 6.5 %collective-permute-start.53 = (f32[1,16,256]{2,1,0:T(8,128)S(1)}, f32[1,16,256]{2,1,0:T(8,128)S(1)}, u32[]{:S(2)}, u32[]{:S(2)}) collective-permute-start(f32[1,16,256]{2,1,0:T(8,128)S(1)} %get-tuple-element.65), channel_id=1, source_target_pairs={{0,8},{8,16},{16,24},{1,9},{9,17},{17,25},{2,10},{10,18},{18,26},{... | collective-permute-start | bytes 49160 | tf_op jit(solution)/shard_map/ppermute | solution.py:19
  289.0 29.2 %collective-permute-start.54 = (f32[10,1,256]{2,1,0:T(1,128)S(1)}, f32[10,1,256]{2,1,0:T(1,128)S(1)}, u32[]{:S(2)}, u32[]{:S(2)}) collective-permute-start(f32[10,1,256]{2,1,0:T(1,128)S(1)} %get-tuple-element.44), channel_id=1, source_target_pairs={{1,0},{2,1},{3,2},{4,3},{5,4},{6,5},{7,6},{9,8},{10,9},{11,10},{12... | collective-permute-start | bytes 30728 | tf_op jit(solution)/shard_map/ppermute | solution.py:22
  290.3 27.9 %collective-permute-start.55 = (f32[10,1,256]{2,1,0:T(1,128)S(1)}, f32[10,1,256]{2,1,0:T(1,128)S(1)}, u32[]{:S(2)}, u32[]{:S(2)}) collective-permute-start(f32[10,1,256]{2,1,0:T(1,128)S(1)} %get-tuple-element.43), channel_id=1, source_target_pairs={{0,1},{1,2},{2,3},{3,4},{4,5},{5,6},{6,7},{8,9},{9,10},{10,11},{11... | collective-permute-start | bytes 30728 | tf_op jit(solution)/shard_map/ppermute | solution.py:19
  349.4 13.1 %all-to-all-start.2 = ((f32[8,1,1,1,4,512]{5,4,3,2,1,0:T(4,128)}), f32[8,1,1,1,4,512]{5,4,3,2,1,0:T(4,128)S(1)}, u32[]{:S(2)}, u32[]{:S(2)}) async-start(f32[8,1,1,1,4,512]{5,4,3,2,1,0:T(4,128)} %constant_dynamic-update-slice_fusion.6), calls=%async_computation.2 | async-start | bytes 131072 | tf_op jit(solution)/shard_map/all_to_all | solution.py:136
  (19 other events, 138.0 us)
